TPU v7x, 128 devices: a whole 4x4x4 slice. The times are simulated.
128 devices in a mesh: section: 2 (over z_lo), patch: 4 (over y), shard: 16 (over z_hi, x, core).
Axes of the slice: x: 4, y: 4, z: 4 (z_hi: 2, z_lo: 2; z = z_hi * 2 + z_lo), core: 2. Of those that a mesh axis runs over, the one named last changes fastest.
Arguments:
- hidden: bfloat16 [32, 1024, 2432], P('shard', 'patch'), may hold values from -6 to 6
- text_kv: bfloat16 [2, 32, 154, 2432], P('section', 'shard'), may hold values from -6 to 6, as said below
- stale_kv: bfloat16 [2, 32, 1024, 2432], P('section', 'shard', 'patch'), may hold values from -6 to 6, as said below
- modulation: float32 [2, 32, 3, 2432], P('section', 'shard'), may hold values from -3 to 3
- score_gain: float32 [2, 64], P('section'), may hold values from 1.5 to 4
- qkv_weight: bfloat16 [2, 2432, 3648], P('section', 'shard'), may hold values from -0.125 to 0.125
- out_weight: bfloat16 [2, 1216, 2432], P('section', None, 'shard'), may hold values from -0.15625 to 0.15625
- final_mod: float32 [32, 2, 2432], P('shard'), may hold values from -3 to 3
- final_weight: bfloat16 [2432, 64], replicated, may hold values from -0.125 to 0.125
- latent: float32 [32, 1024, 64], P('shard', ('patch', 'section')), may hold values from -6 to 6
- step_index: int32 [32], P('shard'), may hold values from 0 to 27
Outputs:
- new_kv: bfloat16 [2, 32, 1024, 2432], P('section', 'shard', 'patch')
- latent_next: float32 [32, 1024, 64], P('shard', ('patch', 'section'))
- denoised: float32 [32, 1024, 64], P('shard', ('patch', 'section'))
Inputs may be any that keep to these rules, and one draw needn't show every extreme that they name: `text_kv`: in every row the first 1216 columns are 19 heads of 64 key features, each head with mean square one up to bfloat16 rounding. `stale_kv`: in every row the first 1216 columns are 19 heads of 64 key features, each head with mean square one up to bfloat16 rounding.
All inputs are finite; a program needn't handle non-finite values.
Results may differ from a plain program's by a relative error of at most 0.008.
Values may be sent and summed in bfloat16 or wider, within the bound.
No kernel may reach another device: no remote copies, remote signals or barrier semaphores. Data moves between devices by JAX's collectives and lax.ppermute only.
A program may use at most 192 MiB of HBM per device.

v0:
```python
import math

import jax
import jax.numpy as jnp
from jax import lax
from jax.sharding import PartitionSpec as P

HEAD = 64
NSTEPS = 28


eps_norm = 1e-06
flow_shift = 3.0


def passed_along(value, axis, steps):
    count = lax.axis_size(axis)
    first, last = (max(0, -steps), min(count, count - steps))
    return lax.ppermute(value, axis, [(source, source + steps) for source in range(first, last)])


def spread(array, axis, root):
    mine = lax.axis_index(axis) == root
    return lax.psum(jnp.where(mine, array, jnp.zeros_like(array)), axis)


def sigma_of(step):
    s = 1.0 - step.astype(jnp.float32) / NSTEPS
    return flow_shift * s / (1.0 + (flow_shift - 1.0) * s)


def modulated(xf, shift, scale):
    mean = jnp.mean(xf, -1, keepdims=True)
    cent = xf - mean
    var = jnp.mean(cent * cent, -1, keepdims=True)
    return cent * lax.rsqrt(var + eps_norm) * (1.0 + scale) + shift


def attend_one(query, keys_all, width, heads):
    count = keys_all.shape[0]
    keys = keys_all[:, :width].reshape(count, heads, HEAD)
    values = keys_all[:, width:].reshape(count, heads, HEAD)
    scores = jnp.einsum("qhe,khe->hqk", query, keys, preferred_element_type=jnp.float32)
    expo = jnp.exp(scores)
    total = jnp.sum(expo, -1)
    weights = expo.astype(jnp.bfloat16)
    mixed = jnp.einsum("hqk,khe->qhe", weights, values, preferred_element_type=jnp.float32)
    mixed = mixed / jnp.transpose(total)[:, :, None]
    return mixed.reshape(query.shape[0], width).astype(jnp.bfloat16)


def run_layer(x, stale_all, text_one, mod_one, gain, w_qkv, w_out, patch_index):
    requests, rows = (x.shape[0], x.shape[1])
    width = w_out.shape[0]
    heads = width // HEAD
    xf = x.astype(jnp.float32)
    normed = modulated(xf, mod_one[:, 0:1, :], mod_one[:, 1:2, :]).astype(jnp.bfloat16)
    proj_in = jnp.einsum("rid,dc->ric", normed, w_qkv, preferred_element_type=jnp.float32)
    q = proj_in[..., :width].reshape(requests, rows, heads, HEAD)
    k = proj_in[..., width : 2 * width].reshape(requests, rows, heads, HEAD)
    v = proj_in[..., 2 * width :]
    q_hat = q * lax.rsqrt(jnp.mean(q * q, -1, keepdims=True) + eps_norm)
    k_hat = k * lax.rsqrt(jnp.mean(k * k, -1, keepdims=True) + eps_norm)
    fresh = jnp.concatenate(
        [k_hat.reshape(requests, rows, width).astype(jnp.bfloat16), v.astype(jnp.bfloat16)], -1
    )
    query = (q_hat * gain / math.sqrt(HEAD)).astype(jnp.bfloat16)
    mixed = lax.dynamic_update_slice_in_dim(stale_all, fresh, patch_index * rows, 1)
    keys_all = jnp.concatenate([text_one, mixed], 1)

    def per_request(pair):
        return attend_one(pair[0], pair[1], width, heads)

    attn = lax.map(per_request, (query, keys_all))
    proj = jnp.einsum("riw,wd->rid", attn, w_out, preferred_element_type=jnp.float32)
    x_next = (xf + mod_one[:, 2:3, :] * proj).astype(jnp.bfloat16)
    return (x_next, fresh)


def on_device(
    hidden,
    text_kv,
    stale_kv,
    modulation,
    score_gain,
    qkv_weight,
    out_weight,
    final_mod,
    final_weight,
    latent,
    step_index,
):
    w_qkv, w_out = (
        lax.all_gather(qkv_weight[0], "shard", axis=0, tiled=True),
        lax.all_gather(out_weight[0], "shard", axis=1, tiled=True),
    )
    stale_all = lax.all_gather(stale_kv[0], "patch", axis=1, tiled=True)
    section = lax.axis_index("section")
    patch_index = lax.axis_index("patch")

    def compute(x):
        return run_layer(
            x, stale_all, text_kv[0], modulation[0], score_gain[0], w_qkv, w_out, patch_index
        )

    def passing(x):
        return (x, jnp.zeros(stale_kv.shape[1:], jnp.bfloat16))

    first, fresh_first = lax.cond(section == 0, compute, passing, hidden)
    arrived = passed_along(first, "section", 1)
    last, fresh_last = lax.cond(section == 1, compute, passing, arrived)
    fresh = jnp.where(section == 0, fresh_first, fresh_last)
    final = modulated(last.astype(jnp.float32), final_mod[:, 0:1, :], final_mod[:, 1:2, :]).astype(
        jnp.bfloat16
    )
    velocity = jnp.einsum("rid,dc->ric", final, final_weight, preferred_element_type=jnp.float32)
    half = latent.shape[1]
    shared = spread(velocity.astype(jnp.bfloat16), "section", 1).astype(velocity.dtype)
    velocity_mine = lax.dynamic_slice_in_dim(shared, section * half, half, 1)
    sig = sigma_of(step_index)[:, None, None]
    sig_next = sigma_of(step_index + 1)[:, None, None]
    latent_next = latent + (sig_next - sig) * velocity_mine
    denoised = latent - sig * velocity_mine
    return (fresh[None], latent_next, denoised)


def solution(mesh):
    in_specs = (
        P("shard", "patch", None),
        P("section", "shard", None, None),
        P("section", "shard", "patch", None),
        P("section", "shard", None, None),
        P("section", None),
        P("section", "shard", None),
        P("section", None, "shard"),
        P("shard", None, None),
        P(),
        P("shard", ("patch", "section"), None),
        P("shard"),
    )
    out_specs = (
        P("section", "shard", "patch", None),
        P("shard", ("patch", "section"), None),
        P("shard", ("patch", "section"), None),
    )
    return jax.shard_map(
        on_device, mesh=mesh, in_specs=in_specs, out_specs=out_specs, check_vma=False
    )
```

profile of v0, /device:TPU:0, one launch (start us, length us, event | category | flops | bytes accessed | tf_op | source)
XLA Modules:
  0.0 642.5 jit_solution(3232019068005679391)
XLA Ops:
  7.2 0.0 copy-start
  7.2 0.0 all-gather.11.cloned.1.call-start
  7.2 0.7 all-gather.11.cloned.1.call-update
  7.9 0.0 copy-start.2
  7.9 0.0 copy-start.7
  7.9 0.0 all-gather.9.cloned.1.call-start
  8.0 4.5 copy.28
  12.5 0.0 all-gather.9.cloned.1.call-update
  12.5 0.0 all-gather.7.cloned.1.call-start
  12.5 0.7 all-gather.7.cloned.1.call-update
  13.2 0.0 all-reduce.2.cloned.1.call-start
  13.3 63.5 %all-gather.11.cloned.1.call-done = bf16[1,1216,2432]{1,2,0:T(8,128)(2,1)} async-done(((bf16[1,1216,152]{1,2,0:T(8,128)(2,1)}), bf16[1,1216,2432]{1,2,0:T(8,128)(2,1)}) %all-gather.11.cloned.1.call-update) | async-done | bytes 5914640 | tf_op jit(solution)/shard_map/all_gather | solution.py:95
  76.8 101.3 %all-gather.9.cloned.1.call-done = bf16[1,2,1024,2432]{2,3,1,0:T(8,128)(2,1)} async-done(((bf16[1,2,256,2432]{2,3,1,0:T(8,128)(2,1)}), bf16[1,2,1024,2432]{2,3,1,0:T(8,128)(2,1)}) %all-gather.9.cloned.1.call-update) | async-done | bytes 9961488 | tf_op jit(solution)/shard_map/all_gather | solution.py:97
  178.1 119.1 %all-gather.7.cloned.1.call-done = bf16[1,2432,3648]{2,1,0:T(8,128)(2,1)} async-done(((bf16[1,152,3648]{2,1,0:T(8,128)(2,1)}), bf16[1,2432,3648]{2,1,0:T(8,128)(2,1)}) %all-gather.7.cloned.1.call-update) | async-done | bytes 17743888 | tf_op jit(solution)/shard_map/all_gather | solution.py:94
  297.2 0.0 copy-start.9
  297.2 129.6 %conditional.2 = (bf16[2,256,2432]{2,1,0:T(8,128)(2,1)S(1)}, bf16[2,256,2432]{2,1,0:T(8,128)(2,1)}) conditional(s32[]{:T(128)} %convert_element_type.88, bf16[2,256,2432]{2,1,0:T(8,128)(2,1)S(1)} %copy-done.2, (bf16[2,256,2432]{2,1,0:T(8,128)(2,1)S(1)}, f32[1,2,3,2432]{3,1,2,0:T(2,128)S(1)}, bf16[2432,3648]{1,0:T(8,128)(2,1)}, f32[1,64]{1,0:T(1,128)S(1)}, ...), branch_computations={%region_0.0_spmd, %region_1.9_spmd} | conditional | flops 13646128128 | bytes 220811024 | solution.py:109
  297.2 0.4 convert_reduce_fusion
  297.6 0.8 fusion.15
  298.4 0.6 slice_bitcast_fusion.1
  299.1 16.5 %fusion.6 = f32[2,256,3648]{1,2,0:T(8,128)} fusion(bf16[2432,3648]{1,0:T(8,128)(2,1)} %get-tuple-element.139, bf16[2,256,2432]{2,1,0:T(8,128)(2,1)S(1)} %get-tuple-element.71, f32[2,2432]{1,0:T(2,128)S(1)} %get-tuple-element.182, f32[2,2432]{1,0:T(2,128)S(1)} %get-tuple-element.183, f32[2,256]{1,0:T(2,128)S(1)} %add_rsqrt_fusion.2, ...), kind=kOutput, calls=%fused_computation.11 | convolution fusion | flops 9092333568 | bytes 27748352 | tf_op jit(solution)/shard_map/cond/branch_1_fun/rid,dc->ric/dot_general | solution.py:58
  315.6 3.3 slice_multiply_fusion
  318.9 2.0 reduce_sum.99
  320.9 4.7 fusion.76
  325.5 2.9 slice.91
  328.4 8.8 %copy.62 = bf16[2,1024,2432]{1,2,0:T(8,128)(2,1)} copy(bf16[2,1024,2432]{1,2,0:T(8,128)(2,1)} %get-tuple-element.74) | data formatting | bytes 19922944 | tf_op jit(solution)/shard_map/cond
  337.2 4.3 pad_maximum_fusion.1
  341.6 5.8 copy.30
  347.3 13.1 %pad_maximum_fusion = bf16[2,1178,2432]{1,2,0:T(8,128)(2,1)} fusion(bf16[2,1024,2432]{1,2,0:T(8,128)(2,1)} %get-tuple-element.180, bf16[2,154,2432]{1,2,0:T(8,128)(2,1)} %bitcast.147), kind=kLoop, calls=%fused_computation.13 | loop fusion | flops 22919168 | bytes 22919168 | tf_op jit(solution)/shard_map/cond/branch_1_fun/concatenate | solution.py:69
  360.4 0.3 multiply_reduce_fusion
  360.8 1.5 multiply_convert_fusion
  362.3 52.4 %while.18 = (s32[]{:T(128)}, bf16[2,256,1216]{1,2,0:T(8,128)(2,1)}, bf16[2,1178,2432]{1,2,0:T(8,128)(2,1)}, bf16[2,256,19,64]{1,3,2,0:T(8,128)(2,1)}, s32[]{:T(128)}) while((s32[]{:T(128)}, bf16[2,256,1216]{1,2,0:T(8,128)(2,1)}, bf16[2,1178,2432]{1,2,0:T(8,128)(2,1)}, bf16[2,256,19,64]{1,3,2,0:T(8,128)(2,1)}, s32[]{:T(128)}) %tuple.88), condition=%wide.region_8.8_spmd, body=%wide.region_6.7_spmd.sunk | while | flops 1478904064 | bytes 82245984 | solution.py:74
  362.8 3.2 dynamic-slice_bitcast_fusion.5
  366.0 0.4 fusion.96
  366.4 0.9 copy-done.5
  367.3 9.7 %exponential_reduce_fusion.5 = (f32[19,256]{1,0:T(8,128)S(1)}, f32[19,256,1178]{1,2,0:T(8,128)}) fusion(bf16[1178,19,64]{0,2,1:T(8,128)(2,1)S(1)} %bitcast.134, bf16[2,256,19,64]{1,3,2,0:T(8,128)(2,1)S(1)} %copy-done.5, s32[]{:T(128)} %get-tuple-element.287), kind=kOutput, calls=%fused_computation.clone.1 | convolution fusion | flops 739138304 | bytes 26674180 | tf_op jit(solution)/shard_map/cond/branch_1_fun/while/body/eval_jaxpr/qhe,khe->hqk/dot_general | solution.py:43
  376.9 10.9 %divide_convert_fusion.5 = bf16[256,19,64]{0,2,1:T(8,128)(2,1)S(1)} fusion(bf16[1178,19,64]{0,2,1:T(8,128)(2,1)S(1)} %bitcast.136, f32[19,256,1178]{1,2,0:T(8,128)} %get-tuple-element.265, f32[256,19]{0,1:T(8,128)S(1)} %bitcast.150), kind=kOutput, calls=%fused_computation.5.clone.1 | convolution fusion | flops 739765760 | bytes 26426112 | tf_op jit(solution)/shard_map/cond/branch_1_fun/while/body/eval_jaxpr/hqk,khe->qhe/dot_general | solution.py:47
  387.9 0.9 constant_dynamic-update-slice_fusion.7
  388.7 3.2 dynamic-slice_bitcast_fusion.5
  391.9 0.0 copy-start.5
  391.9 0.4 fusion.96
  392.3 0.9 copy-done.5
  393.2 9.7 %exponential_reduce_fusion.5 = (f32[19,256]{1,0:T(8,128)S(1)}, f32[19,256,1178]{1,2,0:T(8,128)}) fusion(bf16[1178,19,64]{0,2,1:T(8,128)(2,1)S(1)} %bitcast.134, bf16[2,256,19,64]{1,3,2,0:T(8,128)(2,1)S(1)} %copy-done.5, s32[]{:T(128)} %get-tuple-element.287), kind=kOutput, calls=%fused_computation.clone.1 | convolution fusion | flops 739138304 | bytes 26674180 | tf_op jit(solution)/shard_map/cond/branch_1_fun/while/body/eval_jaxpr/qhe,khe->hqk/dot_general | solution.py:43
  402.9 10.9 %divide_convert_fusion.5 = bf16[256,19,64]{0,2,1:T(8,128)(2,1)S(1)} fusion(bf16[1178,19,64]{0,2,1:T(8,128)(2,1)S(1)} %bitcast.136, f32[19,256,1178]{1,2,0:T(8,128)} %get-tuple-element.265, f32[256,19]{0,1:T(8,128)S(1)} %bitcast.150), kind=kOutput, calls=%fused_computation.5.clone.1 | convolution fusion | flops 739765760 | bytes 26426112 | tf_op jit(solution)/shard_map/cond/branch_1_fun/while/body/eval_jaxpr/hqk,khe->qhe/dot_general | solution.py:47
  413.8 0.9 constant_dynamic-update-slice_fusion.7
  414.7 7.6 %fusion.19 = bf16[2,256,2432]{2,1,0:T(8,128)(2,1)S(1)} fusion(bf16[2,256,2432]{2,1,0:T(8,128)(2,1)S(1)} %get-tuple-element.71, bf16[2,256,1216]{1,2,0:T(8,128)(2,1)} %get-tuple-element.78, bf16[1216,2432]{0,1:T(8,128)(2,1)} %get-tuple-element.144, f32[2,2432]{1,0:T(2,128)S(1)} %copy-done.10), kind=kOutput, calls=%fused_computation.26 | convolution fusion | flops 3033268224 | bytes 12160000 | tf_op jit(solution)/shard_map/cond/branch_1_fun/riw,wd->rid/dot_general | solution.py:75
  422.3 4.3 copy.46
  426.8 1.5 copy-done.1
  428.3 1.4 collective-permute-start
  429.7 0.6 divide_subtract_fusion
  430.4 0.6 copy_bitcast_fusion
  431.0 52.9 %collective-permute-done = bf16[2,256,2432]{2,1,0:T(8,128)(2,1)S(1)} collective-permute-done((bf16[2,256,2432]{2,1,0:T(8,128)(2,1)}, bf16[2,256,2432]{2,1,0:T(8,128)(2,1)S(1)}, u32[]{:S(2)}, u32[]{:S(2)}) %collective-permute-start) | collective-permute-done | bytes 2490400 | tf_op jit(solution)/shard_map/ppermute | solution.py:19
  483.9 4.3 conditional.3
  483.9 1.6 broadcast.161.clone
  488.2 0.0 copy-start.12
  488.2 0.0 copy-start.13
  488.2 0.4 convert_reduce_fusion.2
  488.6 0.8 fusion.60
  489.5 1.8 fusion.69
  491.3 0.0 all-reduce.2.cloned.1.call-update
  491.3 0.0 copy-start.8
  491.4 3.4 select_bitcast_fusion
  494.8 139.3 %all-reduce.2.cloned.1.call-done = bf16[2,256,64]{1,2,0:T(8,128)(2,1)} async-done(((bf16[2,256,64]{1,2,0:T(8,128)(2,1)}), bf16[2,256,64]{1,2,0:T(8,128)(2,1)}) %all-reduce.2.cloned.1.call-update) | async-done | bytes 65552 | tf_op jit(solution)/shard_map/psum | solution.py:24
  634.1 0.0 copy-done.8
  634.1 1.5 fusion.73
  (28 shorter events, 0.1 us)
Async XLA Ops:
  7.2 482.3 %copy-start = (bf16[2432,64]{0,1:T(8,128)(2,1)S(1)}, bf16[2432,64]{0,1:T(8,128)(2,1)}, u32[]{:S(2)}) copy-start(bf16[2432,64]{0,1:T(8,128)(2,1)} %param.27) | copy-start | bytes 933892
  7.2 69.6 %all-gather.11.cloned.1.call-start = ((), (), s32[]{:S(2)}) async-start(), calls=%async_computation.3 | async-start | bytes 6615040 | tf_op jit(solution)/shard_map/all_gather | solution.py:95
  7.9 289.3 %copy-start.2 = (bf16[2,256,2432]{2,1,0:T(8,128)(2,1)S(1)}, bf16[2,256,2432]{2,1,0:T(8,128)(2,1)}, u32[]{:S(2)}) copy-start(bf16[2,256,2432]{2,1,0:T(8,128)(2,1)} %param.19) | copy-start | bytes 7471108
  7.9 289.3 %copy-start.7 = (f32[1,2,3,2432]{3,1,2,0:T(2,128)S(1)}, f32[1,2,3,2432]{3,1,2,0:T(2,128)}, u32[]{:S(2)}) copy-start(f32[1,2,3,2432]{3,1,2,0:T(2,128)} %param.22) | copy-start | bytes 175108
  7.9 289.3 %copy-start.14 = (f32[1,64]{1,0:T(1,128)S(1)}, f32[1,64]{1,0:T(1,128)}, u32[]{:S(2)}) copy-start(f32[1,64]{1,0:T(1,128)} %param.23) | copy-start | bytes 772
  7.9 170.2 %all-gather.9.cloned.1.call-start = ((), (), s32[]{:S(2)}) async-start(), calls=%async_computation.2 | async-start | bytes 12451840 | tf_op jit(solution)/shard_map/all_gather | solution.py:97
  12.5 284.7 %all-gather.7.cloned.1.call-start = ((), (), s32[]{:S(2)}) async-start(), calls=%async_computation.1 | async-start | bytes 19183616 | tf_op jit(solution)/shard_map/all_gather | solution.py:94
  13.2 620.8 %all-reduce.2.cloned.1.call-start = ((), (), s32[]{:S(2)}) async-start(), calls=%async_computation | async-start | bytes 131072 | tf_op jit(solution)/shard_map/psum | solution.py:24
  297.2 132.5 %copy-start.17 = (s32[2]{0:T(128)S(1)}, s32[2]{0:T(128)}, u32[]{:S(2)}) copy-start(s32[2]{0:T(128)} %param.29) | copy-start | bytes 28
  297.2 133.1 %copy-start.9 = (f32[2,2,2432]{2,1,0:T(2,128)S(1)}, f32[2,2,2432]{2,1,0:T(2,128)}, u32[]{:S(2)}) copy-start(f32[2,2,2432]{2,1,0:T(2,128)} %param.26) | copy-start | bytes 116740
  347.3 13.1 %copy-start.3 = (f32[2,256,1216]{1,2,0:T(8,128)S(1)}, f32[2,256,1216]{1,2,0:T(8,128)}, u32[]{:S(2)}) copy-start(f32[2,256,1216]{1,2,0:T(8,128)} %get-tuple-element.177) | copy-start | bytes 7471108 | tf_op jit(solution)/shard_map/cond
  362.3 52.4 %copy-start.10 = (f32[2,2432]{1,0:T(2,128)S(1)}, f32[2,2432]{1,0:T(2,128)}, u32[]{:S(2)}) copy-start(f32[2,2432]{1,0:T(2,128)} %get-tuple-element.181) | copy-start | bytes 58372 | tf_op jit(solution)/shard_map/cond
  366.0 1.3 copy-start.5
  391.9 1.3 copy-start.5
  426.8 1.5 copy-start.1
  428.3 55.6 %collective-permute-start = (bf16[2,256,2432]{2,1,0:T(8,128)(2,1)}, bf16[2,256,2432]{2,1,0:T(8,128)(2,1)S(1)}, u32[]{:S(2)}, u32[]{:S(2)}) collective-permute-start(bf16[2,256,2432]{2,1,0:T(8,128)(2,1)} %copy-done.1), channel_id=1, source_target_pairs={{0,64},{1,65},{2,66},{3,67},{4,68},{5,69},{6,70},{7,71},{8,72},{9,... | collective-permute-start | bytes 7471112 | tf_op jit(solution)/shard_map/ppermute | solution.py:19
  488.2 1.2 copy-start.12
  488.2 1.2 copy-start.13
  491.3 142.7 %copy-start.8 = (f32[2,128,64]{1,2,0:T(8,128)S(1)}, f32[2,128,64]{1,2,0:T(8,128)}, u32[]{:S(2)}) copy-start(f32[2,128,64]{1,2,0:T(8,128)} %param.28) | copy-start | bytes 196612
  491.3 142.7 %copy-start.15 = (f32[2]{0:T(128)S(1)}, f32[2]{0:T(128)}, u32[]{:S(2)}) copy-start(f32[2]{0:T(128)} %get-tuple-element.171) | copy-start | bytes 28
  491.3 142.7 %copy-start.16 = (f32[2]{0:T(128)S(1)}, f32[2]{0:T(128)}, u32[]{:S(2)}) copy-start(f32[2]{0:T(128)} %get-tuple-element.172) | copy-start | bytes 28
Sparse Core Ops, SparseCore 0:
  10.4 66.4 all-gather.10
  79.0 99.0 all-gather.8
  180.7 116.4 all-gather.6
  491.4 142.5 all-reduce.1
where the time goes:
time: 652 us; the launch traced here: 643 us
  waiting for transfers between devices  477 us (73%)
  matrix products  67.2 us (10%)
  local copies, waits for them, and re-layouts  40.7 us (6%)
  other arithmetic  37.8 us (6%)
  between operations  14.4 us (2%)
    psum x1, waiting for transfers between devices, spread(): return lax.psum(jnp.where(mine, array, jnp.zeros_like(array)), axis)  139 us
    all_gather x1, waiting for transfers between devices, on_device(): lax.all_gather(qkv_weight[0], 'shard', axis=0, tiled=True)  119 us
    all_gather x1, waiting for transfers between devices, on_device(): stale_all = lax.all_gather(stale_kv[0], 'patch', axis=1, tiled=True)  101 us
    all_gather x1, waiting for transfers between devices, on_device(): lax.all_gather(out_weight[0], 'shard', axis=1, tiled=True)  63.5 us
    ppermute x1, waiting for transfers between devices, passed_along(): lax.ppermute(value, axis, [(source, source + steps) for source in range(f...  52.9 us
    dot_general x2, matrix products, attend_one(): jnp.einsum('hqk,khe->qhe', weights, values, preferred_element_type=jnp.fl...  21.8 us
    dot_general x2, matrix products, attend_one(): jnp.einsum('qhe,khe->hqk', query, keys, preferred_element_type=jnp.float32)  19.4 us
    dot_general x1, matrix products, run_layer(): jnp.einsum('rid,dc->ric', normed, w_qkv, preferred_element_type=jnp.float32)  16.5 us
  transfers between devices with their start and end apart: 5, of which 5 were waited for; matrix products, arithmetic and copies ran while one was open for 1% of the time, Pallas kernels for 0%

commit v1 on v0

v1 whole, which is shorter than its diff:
```python
import math

import jax
import jax.numpy as jnp
from jax import lax
from jax.experimental import pallas as pl
from jax.experimental.pallas import tpu as pltpu
from jax.sharding import PartitionSpec as P

HEAD = 64
NSTEPS = 28
D = 2432
HW = 1216
ROWS = 256
TXT = 154
TXT_PAD = 160
KEYS = 4 * ROWS + TXT_PAD
BLK = 304
ZC = 1280
XC = D - ZC
LANE = 128
NT = 256

eps_norm = 1e-06
flow_shift = 3.0


def sigma_of(step):
    s = 1.0 - step.astype(jnp.float32) / NSTEPS
    return flow_shift * s / (1.0 + (flow_shift - 1.0) * s)


def shard_pairs(flip_z=0, dx=0, flip_core=0):
    pairs = []
    for z in range(2):
        for x in range(4):
            for c in range(2):
                src = z * 8 + x * 2 + c
                dst = (z ^ flip_z) * 8 + ((x + dx) % 4) * 2 + (c ^ flip_core)
                pairs.append((src, dst))
    return pairs


def ring_pairs(step):
    return [(i, (i + step) % 4) for i in range(4)]


def x_shift(value, dx):
    return lax.ppermute(value, "shard", shard_pairs(dx=dx))


def z_flip(value):
    return lax.ppermute(value, "shard", shard_pairs(flip_z=1))


def core_flip(value):
    return lax.ppermute(value, "shard", shard_pairs(flip_core=1))


def y_shift(value, dy):
    return lax.ppermute(value, "patch", ring_pairs(dy))


def ring_gather(value, shift):
    half = value.shape[0] // 2
    before = shift(value, 1)
    after = shift(value, -1)
    far_low = shift(before[:half], 1)
    far_high = shift(after[half:], -1)
    return before, after, far_low, far_high


def group_scale(p, ones_ref):
    sq = p * p
    hi = sq.astype(jnp.bfloat16)
    lo = (sq - hi.astype(jnp.float32)).astype(jnp.bfloat16)
    ones = ones_ref[...]
    total = jnp.dot(hi, ones, preferred_element_type=jnp.float32) + jnp.dot(
        lo, ones, preferred_element_type=jnp.float32
    )
    return lax.rsqrt(total * (1.0 / HEAD) + eps_norm)


def norm_rows(src_ref, shift_ref, scale_ref, dst_ref):
    step = 32

    def body(i, _):
        r = pl.multiple_of(i * step, step)
        xf = src_ref[pl.ds(r, step), :].astype(jnp.float32)
        mean = jnp.mean(xf, -1, keepdims=True)
        cent = xf - mean
        var = jnp.mean(cent * cent, -1, keepdims=True)
        out = cent * lax.rsqrt(var + eps_norm) * (1.0 + scale_ref[...]) + shift_ref[...]
        dst_ref[pl.ds(r, step), :] = out.astype(jnp.bfloat16)
        return 0

    lax.fori_loop(0, ROWS // step, body, 0)


def layer_kernel(final, *refs):
    (sc, x_ref, mod_ref, fmod_ref, gain_ref, fw_ref) = refs[:6]
    mine = refs[6:13]
    theirs = refs[13:20]
    (st_b, st_a, st_l, st_h, text_ref) = refs[20:25]
    if final:
        vel_ref, fresh_ref = refs[25:27]
        scratch = refs[27:]
        (w_kv, w_q, w_o, kv, normed, qbuf, attn, ones, sems, x_out) = scratch
    else:
        x_out, fresh_ref = refs[25:27]
        scratch = refs[27:]
        (w_kv, w_q, w_o, kv, normed, qbuf, attn, ones, sems) = scratch
    row_of = lambda slot, j: pl.multiple_of(sc[1 + slot * 4 + j], 16)

    def spread_z(pieces, cols, dst, dst_cols, sem):
        zs, zb, za, zl, zh = pieces[:5]
        for j, ref in enumerate((zs, zb, za)):
            for slot in range(2):
                pltpu.make_async_copy(
                    ref.at[pl.ds(slot * BLK, BLK), cols],
                    dst.at[pl.ds(row_of(slot, j), BLK), dst_cols],
                    sem,
                ).start()
        for slot, ref in enumerate((zl, zh)):
            pltpu.make_async_copy(
                ref.at[:, cols], dst.at[pl.ds(row_of(slot, 3), BLK), dst_cols], sem
            ).start()

    def spread_x(pieces, dst, dst_cols, sem):
        for slot in range(2):
            for j in range(4):
                pltpu.make_async_copy(
                    pieces[5 + slot].at[pl.ds(j * BLK, BLK), :],
                    dst.at[pl.ds(row_of(slot, j), BLK), dst_cols],
                    sem,
                ).start()

    def fetch(kv_pieces, oq_pieces):
        spread_z(kv_pieces, pl.ds(0, ZC), w_kv, pl.ds(0, ZC), sems.at[0])
        spread_x(kv_pieces, w_kv, pl.ds(ZC, XC), sems.at[1])
        spread_z(oq_pieces, pl.ds(ZC - LANE, LANE), w_q, pl.ds(0, LANE), sems.at[2])
        spread_x(oq_pieces, w_q, pl.ds(LANE, XC), sems.at[2])

    def fetch_out(oq_pieces):
        spread_z(oq_pieces, pl.ds(0, ZC), w_o, pl.ds(0, ZC), sems.at[4])

    @pl.when(sc[0] == 0)
    def _():
        fetch(mine, theirs)

    @pl.when(sc[0] != 0)
    def _():
        fetch(theirs, mine)

    row = ROWS
    for ref, count in ((st_b, ROWS), (st_a, ROWS), (st_l, ROWS // 2), (st_h, ROWS // 2), (text_ref, TXT_PAD)):
        pltpu.make_async_copy(ref, kv.at[pl.ds(row, count), :], sems.at[3]).start()
        row += count

    @pl.when(sc[0] == 0)
    def _():
        fetch_out(theirs)

    @pl.when(sc[0] != 0)
    def _():
        fetch_out(mine)

    def wait(dst, sem):
        pltpu.make_async_copy(dst, dst, sem).wait()

    norm_rows(x_ref, mod_ref.at[0:1, :], mod_ref.at[1:2, :], normed)
    gi = lax.broadcasted_iota(jnp.int32, (NT, NT), 0) // HEAD
    gj = lax.broadcasted_iota(jnp.int32, (NT, NT), 1) // HEAD
    ones[...] = jnp.where(gi == gj, 1.0, 0.0).astype(jnp.bfloat16)

    wait(w_kv.at[:, pl.ds(0, ZC)], sems.at[0])

    def key_block(j, _):
        c = pl.multiple_of(j * NT, NT)
        p = jnp.dot(normed[...], w_kv[:, pl.ds(c, NT)], preferred_element_type=jnp.float32)
        col = lax.broadcasted_iota(jnp.int32, (ROWS, NT), 1) + c
        out = (p * jnp.where(col < HW, group_scale(p, ones), 1.0)).astype(jnp.bfloat16)
        kv[pl.ds(0, ROWS), pl.ds(c, NT)] = out
        fresh_ref[:, pl.ds(c, NT)] = out
        return 0

    lax.fori_loop(0, ZC // NT, key_block, 0)
    wait(w_kv.at[:, pl.ds(ZC, XC)], sems.at[1])
    vw = 384

    def value_block(j, _):
        c = pl.multiple_of(ZC + j * vw, LANE)
        p = jnp.dot(normed[...], w_kv[:, pl.ds(c, vw)], preferred_element_type=jnp.float32)
        out = p.astype(jnp.bfloat16)
        kv[pl.ds(0, ROWS), pl.ds(c, vw)] = out
        fresh_ref[:, pl.ds(c, vw)] = out
        return 0

    lax.fori_loop(0, XC // vw, value_block, 0)
    wait(w_q, sems.at[2])

    def query_block(j, _):
        c = pl.multiple_of(j * NT, NT)
        p = jnp.dot(normed[...], w_q[:, pl.ds(c, NT)], preferred_element_type=jnp.float32)
        qbuf[:, pl.ds(c, NT)] = p * group_scale(p, ones) * gain_ref[:, pl.ds(c, NT)]
        return 0

    lax.fori_loop(0, ZC // NT, query_block, 0)
    wait(kv.at[pl.ds(ROWS, KEYS - ROWS), :], sems.at[3])

    low = lax.broadcasted_iota(jnp.int32, (ROWS, LANE), 1) < HEAD
    chunks = [(i * ROWS, ROWS) for i in range(4)] + [(4 * ROWS, TXT_PAD)]
    contract = (((1,), (1,)), ((), ()))
    one_rows = jnp.ones((ROWS, LANE), jnp.bfloat16)
    text_rows = jnp.where(
        lax.broadcasted_iota(jnp.int32, (TXT_PAD, LANE), 0) < TXT, 1.0, 0.0
    ).astype(jnp.bfloat16)

    def one_head(q, kc, vc):
        acc = None
        for start, count in chunks:
            k = kv[pl.ds(start, count), pl.ds(kc, LANE)]
            v = kv[pl.ds(start, count), pl.ds(vc, LANE)]
            s = lax.dot_general(q, k, contract, preferred_element_type=jnp.float32)
            w = jnp.exp(s).astype(jnp.bfloat16)
            v_one = jnp.concatenate([v, one_rows if count == ROWS else text_rows], 1)
            part = jnp.dot(w, v_one, preferred_element_type=jnp.float32)
            acc = part if acc is None else acc + part
        return acc[:, :LANE], acc[:, LANE:]

    def pair(i, _):
        c = pl.multiple_of(i * LANE, LANE)
        n = pl.multiple_of(c + LANE, LANE)
        mixed = jnp.where(low, qbuf[:, pl.ds(n, LANE)], qbuf[:, pl.ds(c, LANE)])
        q2 = pltpu.roll(mixed, HEAD, 1)
        q_even = jnp.where(low, q2, 0.0).astype(jnp.bfloat16)
        q_odd = jnp.where(low, 0.0, q2).astype(jnp.bfloat16)
        vc = pl.multiple_of(c + 9 * LANE, LANE)
        vn = pl.multiple_of(c + 10 * LANE, LANE)
        a_even, t_even = one_head(q_even, c, vc)
        a_odd, t_odd = one_head(q_odd, c, vn)
        out = jnp.where(low, a_odd, a_even) / jnp.where(low, t_odd, t_even)
        attn[:, pl.ds(c, LANE)] = pltpu.roll(out, HEAD, 1).astype(jnp.bfloat16)
        return 0

    lax.fori_loop(0, 9, pair, 0)
    q2 = pltpu.roll(qbuf[:, pl.ds(9 * LANE, LANE)], HEAD, 1)
    a_last, t_last = one_head(jnp.where(low, q2, 0.0).astype(jnp.bfloat16), 9 * LANE, 18 * LANE)
    out = jnp.where(low, 0.0, a_last / t_last)
    attn[:, pl.ds(9 * LANE, LANE)] = pltpu.roll(out, HEAD, 1).astype(jnp.bfloat16)

    wait(w_o, sems.at[4])

    def out_block(c, width):
        proj = lax.dot_general(
            attn[...], w_o[pl.ds(c, width), :], contract, preferred_element_type=jnp.float32
        )
        xf = x_ref[:, pl.ds(c, width)].astype(jnp.float32)
        gate = mod_ref[2:3, pl.ds(c, width)]
        x_out[:, pl.ds(c, width)] = (xf + gate * proj).astype(jnp.bfloat16)

    def out_body(j, _):
        out_block(pl.multiple_of(j * NT, NT), NT)
        return 0

    lax.fori_loop(0, D // NT, out_body, 0)
    out_block((D // NT) * NT, D % NT)
    if final:
        norm_rows(x_out, fmod_ref.at[0:1, :], fmod_ref.at[1:2, :], normed)
        vel_ref[...] = jnp.dot(normed[...], fw_ref[...], preferred_element_type=jnp.float32)


def run_layer(scalars, x, mod, fmod, gain, fw, mine, theirs, stale, text, final):
    vmem = pl.BlockSpec(memory_space=pltpu.VMEM)
    hbm = pl.BlockSpec(memory_space=pl.ANY)
    first = (
        jax.ShapeDtypeStruct((ROWS, fw.shape[1]), jnp.float32)
        if final
        else jax.ShapeDtypeStruct((ROWS, D), jnp.bfloat16)
    )
    scratch = [
        pltpu.VMEM((D, D), jnp.bfloat16),
        pltpu.VMEM((D, ZC), jnp.bfloat16),
        pltpu.VMEM((D, ZC), jnp.bfloat16),
        pltpu.VMEM((KEYS, D), jnp.bfloat16),
        pltpu.VMEM((ROWS, D), jnp.bfloat16),
        pltpu.VMEM((ROWS, ZC), jnp.float32),
        pltpu.VMEM((ROWS, ZC), jnp.bfloat16),
        pltpu.VMEM((NT, NT), jnp.bfloat16),
        pltpu.SemaphoreType.DMA((5,)),
    ]
    if final:
        scratch.append(pltpu.VMEM((ROWS, D), jnp.bfloat16))
    return pl.pallas_call(
        lambda *refs: layer_kernel(final, *refs),
        name="last_layer" if final else "first_layer",
        out_shape=(first, jax.ShapeDtypeStruct((ROWS, D), jnp.bfloat16)),
        in_specs=[pl.BlockSpec(memory_space=pltpu.SMEM)] + [vmem] * 5 + [hbm] * 19,
        out_specs=(vmem, vmem),
        scratch_shapes=scratch,
        compiler_params=pltpu.CompilerParams(vmem_limit_bytes=56 << 20),
    )(scalars, x, mod, fmod, gain, fw, *mine, *theirs, *stale, text)


def on_device(
    hidden,
    text_kv,
    stale_kv,
    modulation,
    score_gain,
    qkv_weight,
    out_weight,
    final_mod,
    final_weight,
    latent,
    step_index,
):
    section = lax.axis_index("section")
    shard = lax.axis_index("shard")
    z_hi, x_at, core = shard // 8, (shard // 2) % 4, shard % 2

    qkv = qkv_weight[0]
    half_kv = qkv[:, HW:]
    half_oq = jnp.concatenate([out_weight[0].T, qkv[:, :HW]], 1)
    keep = jnp.where(core == 0, half_kv, half_oq)
    give = jnp.where(core == 0, half_oq, half_kv)
    got = core_flip(give)
    block = jnp.concatenate(
        [jnp.where(core == 0, keep, got), jnp.where(core == 0, got, keep)], 0
    )
    block_z, block_x = block[:, :ZC], block[:, ZC:]
    pair_z = jnp.concatenate([block_z, z_flip(block_z)], 0)
    four_x = jnp.concatenate([block_x, *ring_gather(block_x, x_shift)], 0)
    mine = (pair_z, *ring_gather(pair_z, x_shift), four_x, z_flip(four_x))
    theirs = tuple(core_flip(piece) for piece in mine)

    stale = [ring_gather(stale_kv[0, r], y_shift) for r in range(2)]
    text = jnp.pad(text_kv[0], ((0, 0), (0, TXT_PAD - TXT), (0, 0)))
    gain = jnp.tile(score_gain[0] * (1.0 / math.sqrt(HEAD)), ZC // HEAD)[None, :]
    rows = [
        ((z_hi ^ slot) * 4 + (x_at + dx) % 4) * BLK for slot in range(2) for dx in (0, 3, 1, 2)
    ]
    scalars = jnp.stack([core, *rows]).astype(jnp.int32)

    def layer(x, r, final):
        return run_layer(
            scalars, x, modulation[0, r], final_mod[r], gain, final_weight,
            mine, theirs, stale[r], text[r], final,
        )

    fresh_first, arrived = [], []
    for r in range(2):
        x_next, fresh = layer(hidden[r], r, False)
        fresh_first.append(fresh)
        arrived.append(lax.ppermute(x_next, "section", [(0, 1)]))
    fresh_out, velocity = [], []
    for r in range(2):
        vel, fresh = layer(arrived[r], r, True)
        velocity.append(vel)
        fresh_out.append(jnp.where(section == 0, fresh_first[r], fresh))
    velocity = jnp.stack(velocity)
    half = latent.shape[1]
    sent = lax.ppermute(velocity[:, :half].astype(jnp.bfloat16), "section", [(1, 0)])
    velocity_mine = jnp.where(section == 0, sent.astype(jnp.float32), velocity[:, half:])
    sig = sigma_of(step_index)[:, None, None]
    sig_next = sigma_of(step_index + 1)[:, None, None]
    latent_next = latent + (sig_next - sig) * velocity_mine
    denoised = latent - sig * velocity_mine
    return (jnp.stack(fresh_out)[None], latent_next, denoised)


def solution(mesh):
    in_specs = (
        P("shard", "patch", None),
        P("section", "shard", None, None),
        P("section", "shard", "patch", None),
        P("section", "shard", None, None),
        P("section", None),
        P("section", "shard", None),
        P("section", None, "shard"),
        P("shard", None, None),
        P(),
        P("shard", ("patch", "section"), None),
        P("shard"),
    )
    out_specs = (
        P("section", "shard", "patch", None),
        P("shard", ("patch", "section"), None),
        P("shard", ("patch", "section"), None),
    )
    return jax.shard_map(
        on_device, mesh=mesh, in_specs=in_specs, out_specs=out_specs, check_vma=False
    )
```

time: 652 us -> 307 us (0.47); the launches traced: 643 us -> 307 us
  waiting for transfers between devices: 477 us -> 107 us
  Pallas kernels: 0 us -> 127 us
  matrix products: 67.2 us -> 0 us
  starting transfers between devices: 1.59 us -> 43.8 us
  other arithmetic: 37.8 us -> 5.8 us
  local copies, waits for them, and re-layouts: 40.7 us -> 21.5 us
  between operations: 14.4 us -> 1.19 us
    all_gather x3 -> x0, waiting for transfers between devices: 284 us -> none  [the longest x1 119 us: on_device(): lax.all_gather(qkv_weight[0], 'shard', axis=0, tiled=True)]
    psum x1 -> x0, waiting for transfers between devices: 139 us -> none  [spread(): return lax.psum(jnp.where(mine, array, jnp.zeros_like(array)), axis)]
    pallas_call x0 -> x4, Pallas kernels: none -> 127 us  [run_layer(): pl.pallas_call(lambda *refs: layer_kernel(final, *refs), name='last_layer...]
    dot_general x7 -> x0, matrix products: 67.2 us -> none  [the longest x2 21.8 us: attend_one(): jnp.einsum('hqk,khe->qhe', weights, values, preferred_element_type=jnp.fl...]
    ppermute x1 -> x29, waiting for transfers between devices: 52.9 us -> 107 us  [the longest x8 55.4 us: y_shift(): return lax.ppermute(value, 'patch', ring_pairs(dy))]
    ppermute x1 -> x29, starting transfers between devices: 1.44 us -> 43.8 us  [the longest x8 16.8 us: y_shift(): return lax.ppermute(value, 'patch', ring_pairs(dy))]
    concatenate x2, other arithmetic: 17.4 us -> 0.15 us  [the longest x1 0.1 us: on_device(): pair_z = jnp.concatenate([block_z, z_flip(block_z)], 0)]
    cond x6 -> x0, local copies, waits for them, and re-layouts: 13.1 us -> none
  transfers between devices with their start and end apart: 5 -> 29, of which waited for: 5 -> 11; matrix products, arithmetic and copies ran while one was open for 1% -> 4% of each run, Pallas kernels for 0% -> 31%
where the time goes in v1:
time: 307 us
  Pallas kernels  127 us (41%)
  waiting for transfers between devices  107 us (35%)
  starting transfers between devices  43.8 us (14%)
  local copies, waits for them, and re-layouts  21.5 us (7%)
  other arithmetic  5.8 us (2%)
    pallas_call x4, Pallas kernels, run_layer(): pl.pallas_call(lambda *refs: layer_kernel(final, *refs), name='last_layer...  127 us
    ppermute x8, waiting for transfers between devices, y_shift(): return lax.ppermute(value, 'patch', ring_pairs(dy))  55.4 us
    ppermute x8, waiting for transfers between devices, x_shift(): return lax.ppermute(value, 'shard', shard_pairs(dx=dx))  46.1 us
    ppermute x8, starting transfers between devices, y_shift(): return lax.ppermute(value, 'patch', ring_pairs(dy))  16.8 us
    unnamed x68, local copies, waits for them, and re-layouts  12.7 us
    ppermute x8, starting transfers between devices, x_shift(): return lax.ppermute(value, 'shard', shard_pairs(dx=dx))  11.7 us
    ppermute x2, starting transfers between devices, z_flip(): return lax.ppermute(value, 'shard', shard_pairs(flip_z=1))  8 us
  transfers between devices with their start and end apart: 29, of which 11 were waited for; matrix products, arithmetic and copies ran while one was open for 4% of the time, Pallas kernels for 31%

profile of v1, /device:TPU:0, one launch (start us, length us, event | category | flops | bytes accessed | tf_op | source)
XLA Modules:
  0.0 306.6 jit_solution(15812513751401129992)
XLA Ops:
  0.7 1.1 slice.104
  1.8 1.8 broadcast_select_fusion.2
  3.7 2.2 collective-permute-done
  5.9 0.8 broadcast_select_fusion
  6.8 1.6 collective-permute-start.6
  8.5 1.7 collective-permute-start.7
  10.2 0.2 slice_bitcast_fusion.2
  10.3 1.7 collective-permute-start.23
  12.1 4.0 %collective-permute-start.1 = (bf16[304,1280]{1,0:T(8,128)(2,1)S(1)}, bf16[304,1280]{1,0:T(8,128)(2,1)S(1)}, u32[]{:S(2)}, u32[]{:S(2)}) collective-permute-start(bf16[304,1280]{1,0:T(8,128)(2,1)S(1)} %fusion.2), channel_id=1, source_target_pairs={{0,8},{1,9},{2,10},{3,11},{4,12},{5,13},{6,14},{7,15},{8,0},{9,1},... | collective-permute-start | bytes 2334728 | tf_op jit(solution)/shard_map/ppermute | solution.py:53
  16.1 9.8 %collective-permute-done.6 = bf16[304,1152]{1,0:T(8,128)(2,1)S(1)} collective-permute-done((bf16[304,1152]{1,0:T(8,128)(2,1)S(1)}, bf16[304,1152]{1,0:T(8,128)(2,1)S(1)}, u32[]{:S(2)}, u32[]{:S(2)}) %collective-permute-start.6) | collective-permute-done | bytes 700448 | tf_op jit(solution)/shard_map/ppermute | solution.py:49
  25.9 0.4 collective-permute-start.8
  26.4 2.9 collective-permute-start.9
  29.5 7.1 %collective-permute-done.8 = bf16[152,1152]{1,0:T(8,128)(2,1)S(1)} collective-permute-done((bf16[152,1152]{1,0:T(8,128)(2,1)S(1)}, bf16[152,1152]{1,0:T(8,128)(2,1)S(1)}, u32[]{:S(2)}, u32[]{:S(2)}) %collective-permute-start.8) | collective-permute-done | bytes 350240 | tf_op jit(solution)/shard_map/ppermute | solution.py:49
  36.7 4.0 %collective-permute-start.10 = (bf16[1216,1152]{1,0:T(8,128)(2,1)S(1)}, bf16[1216,1152]{1,0:T(8,128)(2,1)}, u32[]{:S(2)}, u32[]{:S(2)}) collective-permute-start(bf16[1216,1152]{1,0:T(8,128)(2,1)S(1)} %constant_dynamic-update-slice_fusion.refs_11_), channel_id=1, source_target_pairs={{0,8},{1,9},{2,10},{3,11},{4,12},{5,13},{6,14},{7,15},{8,0},{9,1},... | collective-permute-start | bytes 8405000 | tf_op jit(solution)/shard_map/ppermute | solution.py:53
  40.7 3.0 collective-permute-start.24
  43.7 3.2 %collective-permute-start.19 = (bf16[256,2432]{1,0:T(8,128)(2,1)S(1)}, bf16[256,2432]{1,0:T(8,128)(2,1)S(1)}, u32[]{:S(2)}, u32[]{:S(2)}) collective-permute-start(bf16[256,2432]{1,0:T(8,128)(2,1)S(1)} %get-tuple-element.28), channel_id=1, source_target_pairs={{0,48},{16,0},{32,16},{48,32},{1,49},{17,1},{33,17},{49,33},{2,50}... | collective-permute-start | bytes 3735560 | tf_op jit(solution)/shard_map/ppermute | solution.py:61
  47.1 0.4 collective-permute-start.2
  47.6 24.0 %collective-permute-done.24.refs_21_ = bf16[256,2432]{1,0:T(8,128)(2,1)S(1)} collective-permute-done((bf16[256,2432]{1,0:T(8,128)(2,1)S(1)}, bf16[256,2432]{1,0:T(8,128)(2,1)S(1)}, u32[]{:S(2)}, u32[]{:S(2)}) %collective-permute-start.24) | collective-permute-done | bytes 1245216 | tf_op jit(solution)/shard_map/ppermute | solution.py:61
  71.6 1.0 collective-permute-start.25
  72.6 0.9 collective-permute-done.18.refs_20_
  73.6 3.0 collective-permute-start.3
  76.6 18.8 %collective-permute-done.19.refs_21_ = bf16[256,2432]{1,0:T(8,128)(2,1)S(1)} collective-permute-done((bf16[256,2432]{1,0:T(8,128)(2,1)S(1)}, bf16[256,2432]{1,0:T(8,128)(2,1)S(1)}, u32[]{:S(2)}, u32[]{:S(2)}) %collective-permute-start.19) | collective-permute-done | bytes 1245216 | tf_op jit(solution)/shard_map/ppermute | solution.py:61
  95.4 0.6 collective-permute-start.16
  96.0 3.8 %collective-permute-start.26 = (bf16[128,2432]{1,0:T(8,128)(2,1)S(1)}, bf16[128,2432]{1,0:T(8,128)(2,1)S(1)}, u32[]{:S(2)}, u32[]{:S(2)}) collective-permute-start(bf16[128,2432]{1,0:T(8,128)(2,1)S(1)} %slice.114), channel_id=1, source_target_pairs={{0,48},{16,0},{32,16},{48,32},{1,49},{17,1},{33,17},{49,33},{2,50}... | collective-permute-start | bytes 1867784 | tf_op jit(solution)/shard_map/ppermute | solution.py:61
  99.8 0.4 collective-permute-done.10.refs_12_
  100.3 1.2 slice.107
  101.5 11.7 %collective-permute-done.26.refs_23_ = bf16[128,2432]{1,0:T(8,128)(2,1)S(1)} collective-permute-done((bf16[128,2432]{1,0:T(8,128)(2,1)S(1)}, bf16[128,2432]{1,0:T(8,128)(2,1)S(1)}, u32[]{:S(2)}, u32[]{:S(2)}) %collective-permute-start.26) | collective-permute-done | bytes 622624 | tf_op jit(solution)/shard_map/ppermute | solution.py:61
  113.3 0.8 copy-done.12
  114.1 1.3 fusion
  115.4 1.1 copy-done.3
  116.6 0.5 collective-permute-start.13
  117.1 1.2 slice.108
  118.3 14.7 %collective-permute-done.4.refs_9_ = bf16[304,1280]{1,0:T(8,128)(2,1)} collective-permute-done((bf16[304,1280]{1,0:T(8,128)(2,1)S(1)}, bf16[304,1280]{1,0:T(8,128)(2,1)}, u32[]{:S(2)}, u32[]{:S(2)}) %collective-permute-start.4) | collective-permute-done | bytes 778272 | tf_op jit(solution)/shard_map/ppermute | solution.py:49
  133.0 1.5 collective-permute-start.5
  134.5 1.6 slice_bitcast_fusion.3
  136.1 14.5 %collective-permute-done.5.refs_10_ = bf16[304,1280]{1,0:T(8,128)(2,1)} collective-permute-done((bf16[304,1280]{1,0:T(8,128)(2,1)S(1)}, bf16[304,1280]{1,0:T(8,128)(2,1)}, u32[]{:S(2)}, u32[]{:S(2)}) %collective-permute-start.5) | collective-permute-done | bytes 778272 | tf_op jit(solution)/shard_map/ppermute | solution.py:49
  150.6 1.5 copy-done.1
  152.1 0.5 collective-permute-start.15
  152.6 0.6 copy.31
  153.3 0.7 broadcast_in_dim_tile.3.refs_4_
  153.9 2.0 copy.16.refs_5_
  156.0 0.6 copy.32
  156.6 0.6 stack.57.refs_0_
  157.4 0.3 collective-permute-start.20
  157.6 3.8 %collective-permute-start.21 = (bf16[128,2432]{1,0:T(8,128)(2,1)S(1)}, bf16[128,2432]{1,0:T(8,128)(2,1)S(1)}, u32[]{:S(2)}, u32[]{:S(2)}) collective-permute-start(bf16[128,2432]{1,0:T(8,128)(2,1)S(1)} %slice.112), channel_id=1, source_target_pairs={{0,48},{16,0},{32,16},{48,32},{1,49},{17,1},{33,17},{49,33},{2,50}... | collective-permute-start | bytes 1867784 | tf_op jit(solution)/shard_map/ppermute | solution.py:61
  161.4 0.6 slice_bitcast_fusion.5
  162.0 0.9 copy-done.4
  162.9 30.5 %first_layer.3 = (bf16[256,2432]{1,0:T(8,128)(2,1)}, bf16[256,2432]{1,0:T(8,128)(2,1)}) custom-call(s32[9]{0:T(128)} %stack.57.refs_0_, bf16[256,2432]{1,0:T(8,128)(2,1)} %get-tuple-element.31.refs_1_, f32[3,2432]{1,0:T(4,128)} %bitcast.60, f32[2,2432]{1,0:T(2,128)} %get-tuple-element.39.refs_3_, f32[1,1280]{1,0:T(1,128)} %broadcast_in_dim_tile.3.refs_4_, ...), custom_call_target="tpu_custom_call" | custom-call | tf_op jit(solution)/shard_map/first_layer/pallas_call | solution.py:294
  193.4 3.0 collective-permute-start.27
  196.5 0.8 copy-done.13
  197.3 0.2 copy-done.14
  197.5 30.6 %first_layer.2 = (bf16[256,2432]{1,0:T(8,128)(2,1)}, bf16[256,2432]{1,0:T(8,128)(2,1)}) custom-call(s32[9]{0:T(128)} %stack.57.refs_0_, bf16[256,2432]{1,0:T(8,128)(2,1)} %get-tuple-element.30.refs_1_, f32[3,2432]{1,0:T(4,128)} %bitcast.58, f32[2,2432]{1,0:T(2,128)} %get-tuple-element.38.refs_3_, f32[1,1280]{1,0:T(1,128)} %broadcast_in_dim_tile.3.refs_4_, ...), custom_call_target="tpu_custom_call" | custom-call | tf_op jit(solution)/shard_map/first_layer/pallas_call | solution.py:294
  228.1 1.4 collective-permute-start.22
  229.6 1.0 copy-done.18
  230.7 32.9 %last_layer.3 = (f32[256,64]{1,0:T(8,128)}, bf16[256,2432]{1,0:T(8,128)(2,1)}) custom-call(s32[9]{0:T(128)} %stack.57.refs_0_, bf16[256,2432]{1,0:T(8,128)(2,1)} %copy-done.18, f32[3,2432]{1,0:T(4,128)} %bitcast.61, f32[2,2432]{1,0:T(2,128)} %get-tuple-element.39.refs_3_, f32[1,1280]{1,0:T(1,128)} %broadcast_in_dim_tile.3.refs_4_, ...), custom_call_target="tpu_custom_call" | custom-call | tf_op jit(solution)/shard_map/last_layer/pallas_call | solution.py:294
  263.6 1.1 copy-done.17
  264.7 33.4 %last_layer.2 = (f32[256,64]{1,0:T(8,128)}, bf16[256,2432]{1,0:T(8,128)(2,1)}) custom-call(s32[9]{0:T(128)} %stack.57.refs_0_, bf16[256,2432]{1,0:T(8,128)(2,1)} %copy-done.17, f32[3,2432]{1,0:T(4,128)} %bitcast.59, f32[2,2432]{1,0:T(2,128)} %get-tuple-element.38.refs_3_, f32[1,1280]{1,0:T(1,128)} %broadcast_in_dim_tile.3.refs_4_, ...), custom_call_target="tpu_custom_call" | custom-call | tf_op jit(solution)/shard_map/last_layer/pallas_call | solution.py:294
  298.1 0.9 fusion.4
  298.9 1.3 collective-permute-start.28
  300.3 0.3 select_bitcast_fusion
  300.6 1.7 maximum_bitcast_fusion
  302.3 2.8 collective-permute-done.28
  305.2 0.7 copy.23
  305.9 0.7 copy.24
  (95 shorter events, 1.5 us)
Async XLA Ops:
  0.6 5.3 %copy-start.9 = (bf16[1,152,3648]{2,1,0:T(8,128)(2,1)S(1)}, bf16[1,152,3648]{2,1,0:T(8,128)(2,1)}, u32[]{:S(2)}) copy-start(bf16[1,152,3648]{2,1,0:T(8,128)(2,1)} %param.16) | copy-start | bytes 3326980
  0.6 5.3 %copy-start.15 = (bf16[1,1216,152]{1,2,0:T(8,128)(2,1)S(1)}, bf16[1,1216,152]{1,2,0:T(8,128)(2,1)}, u32[]{:S(2)}) copy-start(bf16[1,1216,152]{1,2,0:T(8,128)(2,1)} %param.17) | copy-start | bytes 1108996
  3.6 2.3 collective-permute-start
  6.7 3.4 %copy-start.10 = (bf16[1,2,256,2432]{3,2,1,0:T(8,128)(2,1)S(1)}, bf16[1,2,256,2432]{3,2,1,0:T(8,128)(2,1)}, u32[]{:S(2)}) copy-start(bf16[1,2,256,2432]{3,2,1,0:T(8,128)(2,1)} %param.13) | copy-start | bytes 7471108
  6.8 19.0 %collective-permute-start.6 = (bf16[304,1152]{1,0:T(8,128)(2,1)S(1)}, bf16[304,1152]{1,0:T(8,128)(2,1)S(1)}, u32[]{:S(2)}, u32[]{:S(2)}) collective-permute-start(bf16[304,1152]{1,0:T(8,128)(2,1)S(1)} %get-tuple-element.25), channel_id=1, source_target_pairs={{0,2},{1,3},{2,4},{3,5},{4,6},{5,7},{6,0},{7,1},{8,10},{9,11},{10,... | collective-permute-start | bytes 2101256 | tf_op jit(solution)/shard_map/ppermute | solution.py:49
  8.5 17.8 %collective-permute-start.7 = (bf16[304,1152]{1,0:T(8,128)(2,1)S(1)}, bf16[304,1152]{1,0:T(8,128)(2,1)S(1)}, u32[]{:S(2)}, u32[]{:S(2)}) collective-permute-start(bf16[304,1152]{1,0:T(8,128)(2,1)S(1)} %get-tuple-element.25), channel_id=1, source_target_pairs={{0,6},{1,7},{2,0},{3,1},{4,2},{5,3},{6,4},{7,5},{8,14},{9,15},{10,... | collective-permute-start | bytes 2101256 | tf_op jit(solution)/shard_map/ppermute | solution.py:49
  10.3 36.8 %collective-permute-start.23 = (bf16[256,2432]{1,0:T(8,128)(2,1)S(1)}, bf16[256,2432]{1,0:T(8,128)(2,1)S(1)}, u32[]{:S(2)}, u32[]{:S(2)}) collective-permute-start(bf16[256,2432]{1,0:T(8,128)(2,1)S(1)} %get-tuple-element.29), channel_id=1, source_target_pairs={{0,16},{16,32},{32,48},{48,0},{1,17},{17,33},{33,49},{49,1},{2,18}... | collective-permute-start | bytes 3735560 | tf_op jit(solution)/shard_map/ppermute | solution.py:61
  12.1 31.6 %collective-permute-start.1 = (bf16[304,1280]{1,0:T(8,128)(2,1)S(1)}, bf16[304,1280]{1,0:T(8,128)(2,1)S(1)}, u32[]{:S(2)}, u32[]{:S(2)}) collective-permute-start(bf16[304,1280]{1,0:T(8,128)(2,1)S(1)} %fusion.2), channel_id=1, source_target_pairs={{0,8},{1,9},{2,10},{3,11},{4,12},{5,13},{6,14},{7,15},{8,0},{9,1},... | collective-permute-start | bytes 2334728 | tf_op jit(solution)/shard_map/ppermute | solution.py:53
  25.9 10.7 %collective-permute-start.8 = (bf16[152,1152]{1,0:T(8,128)(2,1)S(1)}, bf16[152,1152]{1,0:T(8,128)(2,1)S(1)}, u32[]{:S(2)}, u32[]{:S(2)}) collective-permute-start(bf16[152,1152]{1,0:T(8,128)(2,1)S(1)} %slice.109), channel_id=1, source_target_pairs={{0,2},{1,3},{2,4},{3,5},{4,6},{5,7},{6,0},{7,1},{8,10},{9,11},{10,... | collective-permute-start | bytes 1050632 | tf_op jit(solution)/shard_map/ppermute | solution.py:49
  26.4 10.3 %collective-permute-start.9 = (bf16[152,1152]{1,0:T(8,128)(2,1)S(1)}, bf16[152,1152]{1,0:T(8,128)(2,1)S(1)}, u32[]{:S(2)}, u32[]{:S(2)}) collective-permute-start(bf16[152,1152]{1,0:T(8,128)(2,1)S(1)} %slice.110), channel_id=1, source_target_pairs={{0,6},{1,7},{2,0},{3,1},{4,2},{5,3},{6,4},{7,5},{8,14},{9,15},{10,... | collective-permute-start | bytes 1050632 | tf_op jit(solution)/shard_map/ppermute | solution.py:49
  36.7 58.7 %copy-start = (bf16[1216,1152]{1,0:T(8,128)(2,1)}, bf16[1216,1152]{1,0:T(8,128)(2,1)S(1)}, u32[]{:S(2)}) copy-start(bf16[1216,1152]{1,0:T(8,128)(2,1)S(1)} %constant_dynamic-update-slice_fusion.refs_11_) | copy-start | bytes 8404996
  36.7 63.4 %collective-permute-start.10 = (bf16[1216,1152]{1,0:T(8,128)(2,1)S(1)}, bf16[1216,1152]{1,0:T(8,128)(2,1)}, u32[]{:S(2)}, u32[]{:S(2)}) collective-permute-start(bf16[1216,1152]{1,0:T(8,128)(2,1)S(1)} %constant_dynamic-update-slice_fusion.refs_11_), channel_id=1, source_target_pairs={{0,8},{1,9},{2,10},{3,11},{4,12},{5,13},{6,14},{7,15},{8,0},{9,1},... | collective-permute-start | bytes 8405000 | tf_op jit(solution)/shard_map/ppermute | solution.py:53
  40.7 30.8 %collective-permute-start.24 = (bf16[256,2432]{1,0:T(8,128)(2,1)S(1)}, bf16[256,2432]{1,0:T(8,128)(2,1)S(1)}, u32[]{:S(2)}, u32[]{:S(2)}) collective-permute-start(bf16[256,2432]{1,0:T(8,128)(2,1)S(1)} %get-tuple-element.29), channel_id=1, source_target_pairs={{0,48},{16,0},{32,16},{48,32},{1,49},{17,1},{33,17},{49,33},{2,50}... | collective-permute-start | bytes 3735560 | tf_op jit(solution)/shard_map/ppermute | solution.py:61
  43.7 29.8 %collective-permute-start.18 = (bf16[256,2432]{1,0:T(8,128)(2,1)S(1)}, bf16[256,2432]{1,0:T(8,128)(2,1)S(1)}, u32[]{:S(2)}, u32[]{:S(2)}) collective-permute-start(bf16[256,2432]{1,0:T(8,128)(2,1)S(1)} %get-tuple-element.28), channel_id=1, source_target_pairs={{0,16},{16,32},{32,48},{48,0},{1,17},{17,33},{33,49},{49,1},{2,18}... | collective-permute-start | bytes 3735560 | tf_op jit(solution)/shard_map/ppermute | solution.py:61
  43.7 51.6 %collective-permute-start.19 = (bf16[256,2432]{1,0:T(8,128)(2,1)S(1)}, bf16[256,2432]{1,0:T(8,128)(2,1)S(1)}, u32[]{:S(2)}, u32[]{:S(2)}) collective-permute-start(bf16[256,2432]{1,0:T(8,128)(2,1)S(1)} %get-tuple-element.28), channel_id=1, source_target_pairs={{0,48},{16,0},{32,16},{48,32},{1,49},{17,1},{33,17},{49,33},{2,50}... | collective-permute-start | bytes 3735560 | tf_op jit(solution)/shard_map/ppermute | solution.py:61
  47.1 53.2 %copy-start.2 = (bf16[608,1280]{1,0:T(8,128)(2,1)}, bf16[608,1280]{1,0:T(8,128)(2,1)S(1)}, u32[]{:S(2)}) copy-start(bf16[608,1280]{1,0:T(8,128)(2,1)S(1)} %pad_maximum_fusion.refs_6_) | copy-start | bytes 4669444
  47.1 53.0 %copy-start.16 = (bf16[1,2,154,2432]{3,1,2,0:T(2,128)(2,1)S(1)}, bf16[1,2,154,2432]{3,1,2,0:T(2,128)(2,1)}, u32[]{:S(2)}) copy-start(bf16[1,2,154,2432]{3,1,2,0:T(2,128)(2,1)} %param.12) | copy-start | bytes 4494340
  47.1 48.2 %copy-start.5 = (bf16[256,2432]{1,0:T(8,128)(2,1)}, bf16[256,2432]{1,0:T(8,128)(2,1)S(1)}, u32[]{:S(2)}) copy-start(bf16[256,2432]{1,0:T(8,128)(2,1)S(1)} %collective-permute-done.23.refs_20_) | copy-start | bytes 3735556
  47.1 48.9 %collective-permute-start.2 = (bf16[608,1280]{1,0:T(8,128)(2,1)S(1)}, bf16[608,1280]{1,0:T(8,128)(2,1)}, u32[]{:S(2)}, u32[]{:S(2)}) collective-permute-start(bf16[608,1280]{1,0:T(8,128)(2,1)S(1)} %pad_maximum_fusion.refs_6_), channel_id=1, source_target_pairs={{0,2},{1,3},{2,4},{3,5},{4,6},{5,7},{6,0},{7,1},{8,10},{9,11},{10,... | collective-permute-start | bytes 4669448 | tf_op jit(solution)/shard_map/ppermute | solution.py:49
  71.6 28.7 %copy-start.8 = (bf16[256,2432]{1,0:T(8,128)(2,1)}, bf16[256,2432]{1,0:T(8,128)(2,1)S(1)}, u32[]{:S(2)}) copy-start(bf16[256,2432]{1,0:T(8,128)(2,1)S(1)} %collective-permute-done.24.refs_21_) | copy-start | bytes 3735556
  71.6 23.8 %collective-permute-start.25 = (bf16[128,2432]{1,0:T(8,128)(2,1)S(1)}, bf16[128,2432]{1,0:T(8,128)(2,1)}, u32[]{:S(2)}, u32[]{:S(2)}) collective-permute-start(bf16[128,2432]{1,0:T(8,128)(2,1)S(1)} %slice.113), channel_id=1, source_target_pairs={{0,16},{16,32},{32,48},{48,0},{1,17},{17,33},{33,49},{49,1},{2,18}... | collective-permute-start | bytes 1867784 | tf_op jit(solution)/shard_map/ppermute | solution.py:61
  73.6 83.7 %copy-start.6 = (bf16[256,2432]{1,0:T(8,128)(2,1)}, bf16[256,2432]{1,0:T(8,128)(2,1)S(1)}, u32[]{:S(2)}) copy-start(bf16[256,2432]{1,0:T(8,128)(2,1)S(1)} %collective-permute-done.18.refs_20_) | copy-start | bytes 3735556
  73.6 41.8 %collective-permute-start.3 = (bf16[608,1280]{1,0:T(8,128)(2,1)S(1)}, bf16[608,1280]{1,0:T(8,128)(2,1)}, u32[]{:S(2)}, u32[]{:S(2)}) collective-permute-start(bf16[608,1280]{1,0:T(8,128)(2,1)S(1)} %pad_maximum_fusion.refs_6_), channel_id=1, source_target_pairs={{0,6},{1,7},{2,0},{3,1},{4,2},{5,3},{6,4},{7,5},{8,14},{9,15},{10,... | collective-permute-start | bytes 4669448 | tf_op jit(solution)/shard_map/ppermute | solution.py:49
  95.3 62.0 %copy-start.7 = (bf16[256,2432]{1,0:T(8,128)(2,1)}, bf16[256,2432]{1,0:T(8,128)(2,1)S(1)}, u32[]{:S(2)}) copy-start(bf16[256,2432]{1,0:T(8,128)(2,1)S(1)} %collective-permute-done.19.refs_21_) | copy-start | bytes 3735556
  95.3 20.1 %collective-permute-start.11 = (bf16[608,1280]{1,0:T(8,128)(2,1)S(1)}, bf16[608,1280]{1,0:T(8,128)(2,1)S(1)}, u32[]{:S(2)}, u32[]{:S(2)}) collective-permute-start(bf16[608,1280]{1,0:T(8,128)(2,1)S(1)} %pad_maximum_fusion.refs_6_), channel_id=1, source_target_pairs={{0,1},{1,0},{2,3},{3,2},{4,5},{5,4},{6,7},{7,6},{8,9},{9,8},{10,11... | collective-permute-start | bytes 4669448 | tf_op jit(solution)/shard_map/ppermute | solution.py:57
  95.4 55.3 %collective-permute-start.16 = (bf16[1216,1152]{1,0:T(8,128)(2,1)S(1)}, bf16[1216,1152]{1,0:T(8,128)(2,1)S(1)}, u32[]{:S(2)}, u32[]{:S(2)}) collective-permute-start(bf16[1216,1152]{1,0:T(8,128)(2,1)S(1)} %constant_dynamic-update-slice_fusion.refs_11_), channel_id=1, source_target_pairs={{0,1},{1,0},{2,3},{3,2},{4,5},{5,4},{6,7},{7,6},{8,9},{9,8},{10,11... | collective-permute-start | bytes 8405000 | tf_op jit(solution)/shard_map/ppermute | solution.py:57
  96.0 17.2 %collective-permute-start.26 = (bf16[128,2432]{1,0:T(8,128)(2,1)S(1)}, bf16[128,2432]{1,0:T(8,128)(2,1)S(1)}, u32[]{:S(2)}, u32[]{:S(2)}) collective-permute-start(bf16[128,2432]{1,0:T(8,128)(2,1)S(1)} %slice.114), channel_id=1, source_target_pairs={{0,48},{16,0},{32,16},{48,32},{1,49},{17,1},{33,17},{49,33},{2,50}... | collective-permute-start | bytes 1867784 | tf_op jit(solution)/shard_map/ppermute | solution.py:61
  100.1 61.9 %collective-permute-start.17 = (bf16[1216,1152]{1,0:T(8,128)(2,1)}, bf16[1216,1152]{1,0:T(8,128)(2,1)}, u32[]{:S(2)}, u32[]{:S(2)}) collective-permute-start(bf16[1216,1152]{1,0:T(8,128)(2,1)} %collective-permute-done.10.refs_12_), channel_id=1, source_target_pairs={{0,1},{1,0},{2,3},{3,2},{4,5},{5,4},{6,7},{7,6},{8,9},{9,8},{10,11... | collective-permute-start | bytes 8405000 | tf_op jit(solution)/shard_map/ppermute | solution.py:57
  113.2 0.9 copy-start.12
  113.2 19.8 %collective-permute-start.4 = (bf16[304,1280]{1,0:T(8,128)(2,1)S(1)}, bf16[304,1280]{1,0:T(8,128)(2,1)}, u32[]{:S(2)}, u32[]{:S(2)}) collective-permute-start(bf16[304,1280]{1,0:T(8,128)(2,1)S(1)} %slice.107), channel_id=1, source_target_pairs={{0,2},{1,3},{2,4},{3,5},{4,6},{5,7},{6,0},{7,1},{8,10},{9,11},{10,... | collective-permute-start | bytes 2334728 | tf_op jit(solution)/shard_map/ppermute | solution.py:49
  114.1 3.0 copy-start.25
  114.1 20.4 %copy-start.11 = (bf16[2,256,2432]{2,1,0:T(8,128)(2,1)S(1)}, bf16[2,256,2432]{2,1,0:T(8,128)(2,1)}, u32[]{:S(2)}) copy-start(bf16[2,256,2432]{2,1,0:T(8,128)(2,1)} %param.11) | copy-start | bytes 7471108
  115.4 42.0 %collective-permute-start.12 = (bf16[608,1280]{1,0:T(8,128)(2,1)}, bf16[608,1280]{1,0:T(8,128)(2,1)}, u32[]{:S(2)}, u32[]{:S(2)}) collective-permute-start(bf16[608,1280]{1,0:T(8,128)(2,1)} %collective-permute-done.2.refs_7_), channel_id=1, source_target_pairs={{0,1},{1,0},{2,3},{3,2},{4,5},{5,4},{6,7},{7,6},{8,9},{9,8},{10,11... | collective-permute-start | bytes 4669448 | tf_op jit(solution)/shard_map/ppermute | solution.py:57
  115.4 1.1 copy-start.3
  116.6 41.1 %collective-permute-start.13 = (bf16[608,1280]{1,0:T(8,128)(2,1)}, bf16[608,1280]{1,0:T(8,128)(2,1)}, u32[]{:S(2)}, u32[]{:S(2)}) collective-permute-start(bf16[608,1280]{1,0:T(8,128)(2,1)} %collective-permute-done.3.refs_8_), channel_id=1, source_target_pairs={{0,1},{1,0},{2,3},{3,2},{4,5},{5,4},{6,7},{7,6},{8,9},{9,8},{10,11... | collective-permute-start | bytes 4669448 | tf_op jit(solution)/shard_map/ppermute | solution.py:57
  118.3 34.3 %copy-start.27 = (f32[1,64]{1,0:T(1,128)S(1)}, f32[1,64]{1,0:T(1,128)}, u32[]{:S(2)}) copy-start(f32[1,64]{1,0:T(1,128)} %param.15) | copy-start | bytes 772
  133.0 17.6 %collective-permute-start.5 = (bf16[304,1280]{1,0:T(8,128)(2,1)S(1)}, bf16[304,1280]{1,0:T(8,128)(2,1)}, u32[]{:S(2)}, u32[]{:S(2)}) collective-permute-start(bf16[304,1280]{1,0:T(8,128)(2,1)S(1)} %slice.108), channel_id=1, source_target_pairs={{0,6},{1,7},{2,0},{3,1},{4,2},{5,3},{6,4},{7,5},{8,14},{9,15},{10,... | collective-permute-start | bytes 2334728 | tf_op jit(solution)/shard_map/ppermute | solution.py:49
  150.6 11.4 %collective-permute-start.14 = (bf16[304,1280]{1,0:T(8,128)(2,1)}, bf16[304,1280]{1,0:T(8,128)(2,1)}, u32[]{:S(2)}, u32[]{:S(2)}) collective-permute-start(bf16[304,1280]{1,0:T(8,128)(2,1)} %collective-permute-done.4.refs_9_), channel_id=1, source_target_pairs={{0,1},{1,0},{2,3},{3,2},{4,5},{5,4},{6,7},{7,6},{8,9},{9,8},{10,11... | collective-permute-start | bytes 2334728 | tf_op jit(solution)/shard_map/ppermute | solution.py:57
  150.6 1.5 copy-start.1
  152.1 9.9 %collective-permute-start.15 = (bf16[304,1280]{1,0:T(8,128)(2,1)}, bf16[304,1280]{1,0:T(8,128)(2,1)S(1)}, u32[]{:S(2)}, u32[]{:S(2)}) collective-permute-start(bf16[304,1280]{1,0:T(8,128)(2,1)} %collective-permute-done.5.refs_10_), channel_id=1, source_target_pairs={{0,1},{1,0},{2,3},{3,2},{4,5},{5,4},{6,7},{7,6},{8,9},{9,8},{10,11... | collective-permute-start | bytes 2334728 | tf_op jit(solution)/shard_map/ppermute | solution.py:57
  153.9 7.5 %copy-start.26 = (f32[2,2,2432]{2,1,0:T(2,128)S(1)}, f32[2,2,2432]{2,1,0:T(2,128)}, u32[]{:S(2)}) copy-start(f32[2,2,2432]{2,1,0:T(2,128)} %param.18) | copy-start | bytes 116740
  157.4 39.1 %collective-permute-start.20 = (bf16[128,2432]{1,0:T(8,128)(2,1)S(1)}, bf16[128,2432]{1,0:T(8,128)(2,1)S(1)}, u32[]{:S(2)}, u32[]{:S(2)}) collective-permute-start(bf16[128,2432]{1,0:T(8,128)(2,1)S(1)} %slice.111), channel_id=1, source_target_pairs={{0,16},{16,32},{32,48},{48,0},{1,17},{17,33},{33,49},{49,1},{2,18}... | collective-permute-start | bytes 1867784 | tf_op jit(solution)/shard_map/ppermute | solution.py:61
  157.6 38.8 %collective-permute-start.21 = (bf16[128,2432]{1,0:T(8,128)(2,1)S(1)}, bf16[128,2432]{1,0:T(8,128)(2,1)S(1)}, u32[]{:S(2)}, u32[]{:S(2)}) collective-permute-start(bf16[128,2432]{1,0:T(8,128)(2,1)S(1)} %slice.112), channel_id=1, source_target_pairs={{0,48},{16,0},{32,16},{48,32},{1,49},{17,1},{33,17},{49,33},{2,50}... | collective-permute-start | bytes 1867784 | tf_op jit(solution)/shard_map/ppermute | solution.py:61
  162.0 0.9 copy-start.4
  193.4 36.2 %collective-permute-start.27 = (bf16[256,2432]{1,0:T(8,128)(2,1)}, bf16[256,2432]{1,0:T(8,128)(2,1)S(1)}, u32[]{:S(2)}, u32[]{:S(2)}) collective-permute-start(bf16[256,2432]{1,0:T(8,128)(2,1)} %get-tuple-element.15), channel_id=1, source_target_pairs={{0,64},{1,65},{2,66},{3,67},{4,68},{5,69},{6,70},{7,71},{8,72},{9,... | collective-permute-start | bytes 3735560 | tf_op jit(solution)/shard_map/ppermute | solution.py:355
  196.4 0.8 copy-start.13
  196.5 1.0 copy-start.14
  197.5 32.0 %copy-start.24 = (f32[2,128,64]{1,2,0:T(8,128)S(1)}, f32[2,128,64]{1,2,0:T(8,128)}, u32[]{:S(2)}) copy-start(f32[2,128,64]{1,2,0:T(8,128)} %param.20) | copy-start | bytes 196612
  197.5 32.1 %copy-start.28 = (s32[2]{0:T(128)S(1)}, s32[2]{0:T(128)}, u32[]{:S(2)}) copy-start(s32[2]{0:T(128)} %param.21) | copy-start | bytes 28
  228.1 35.5 %collective-permute-start.22 = (bf16[256,2432]{1,0:T(8,128)(2,1)}, bf16[256,2432]{1,0:T(8,128)(2,1)S(1)}, u32[]{:S(2)}, u32[]{:S(2)}) collective-permute-start(bf16[256,2432]{1,0:T(8,128)(2,1)} %get-tuple-element.12), channel_id=1, source_target_pairs={{0,64},{1,65},{2,66},{3,67},{4,68},{5,69},{6,70},{7,71},{8,72},{9,... | collective-permute-start | bytes 3735560 | tf_op jit(solution)/shard_map/ppermute | solution.py:355
  229.6 1.0 copy-start.18
  263.5 34.5 %copy-start.22 = (f32[256,64]{1,0:T(8,128)S(1)}, f32[256,64]{1,0:T(8,128)}, u32[]{:S(2)}) copy-start(f32[256,64]{1,0:T(8,128)} %get-tuple-element.18) | copy-start | bytes 196612
  263.6 36.7 %copy-start.19 = (bf16[256,2432]{1,0:T(8,128)(2,1)S(1)}, bf16[256,2432]{1,0:T(8,128)(2,1)}, u32[]{:S(2)}) copy-start(bf16[256,2432]{1,0:T(8,128)(2,1)} %get-tuple-element.14) | copy-start | bytes 3735556
  263.6 36.7 %copy-start.20 = (bf16[256,2432]{1,0:T(8,128)(2,1)S(1)}, bf16[256,2432]{1,0:T(8,128)(2,1)}, u32[]{:S(2)}) copy-start(bf16[256,2432]{1,0:T(8,128)(2,1)} %get-tuple-element.11) | copy-start | bytes 3735556
  263.6 36.7 %copy-start.21 = (bf16[256,2432]{1,0:T(8,128)(2,1)S(1)}, bf16[256,2432]{1,0:T(8,128)(2,1)}, u32[]{:S(2)}) copy-start(bf16[256,2432]{1,0:T(8,128)(2,1)} %get-tuple-element.16) | copy-start | bytes 3735556
  263.6 1.1 copy-start.17
  298.9 6.2 %collective-permute-start.28 = (bf16[2,128,64]{2,1,0:T(8,128)(2,1)S(1)}, bf16[2,128,64]{2,1,0:T(8,128)(2,1)S(1)}, u32[]{:S(2)}, u32[]{:S(2)}) collective-permute-start(bf16[2,128,64]{2,1,0:T(8,128)(2,1)S(1)} %fusion.4), channel_id=1, source_target_pairs={{64,0},{65,1},{66,2},{67,3},{68,4},{69,5},{70,6},{71,7},{72,8},{73... | collective-permute-start | bytes 98312 | tf_op jit(solution)/shard_map/ppermute | solution.py:363
  300.6 4.5 %copy-start.23 = (f32[256,64]{1,0:T(8,128)S(1)}, f32[256,64]{1,0:T(8,128)}, u32[]{:S(2)}) copy-start(f32[256,64]{1,0:T(8,128)} %get-tuple-element.17) | copy-start | bytes 196612

commit v2 on v1

--- a/solution.py
+++ b/solution.py
@@ -61,13 +61,27 @@
     return lax.ppermute(value, "patch", ring_pairs(dy))
 
 
-def ring_gather(value, shift):
-    half = value.shape[0] // 2
-    before = shift(value, 1)
-    after = shift(value, -1)
-    far_low = shift(before[:half], 1)
-    far_high = shift(after[half:], -1)
-    return before, after, far_low, far_high
+def x_relay(value):
+    pairs = []
+    for z in range(2):
+        for x in range(4):
+            for c in range(2):
+                dx = 1 if c == 0 else -1
+                pairs.append((z * 8 + x * 2 + c, z * 8 + ((x + dx) % 4) * 2 + c))
+    return lax.ppermute(value, "shard", pairs)
+
+
+def y_relay(value):
+    pairs = []
+    for y in range(4):
+        for k in range(16):
+            dy = 1 if k % 2 == 0 else -1
+            pairs.append((y * 16 + k, ((y + dy) % 4) * 16 + k))
+    return lax.ppermute(value, ("patch", "shard"), pairs)
+
+
+def after(value, *earlier):
+    return lax.optimization_barrier((value, *earlier))[0]
 
 
 def group_scale(p, ones_ref):
@@ -97,43 +111,46 @@
     lax.fori_loop(0, ROWS // step, body, 0)
 
 
-def layer_kernel(final, *refs):
+def layer_kernel(final, req, *refs):
     (sc, x_ref, mod_ref, fmod_ref, gain_ref, fw_ref) = refs[:6]
-    mine = refs[6:13]
-    theirs = refs[13:20]
-    (st_b, st_a, st_l, st_h, text_ref) = refs[20:25]
+    mod_ref, fmod_ref = mod_ref.at[req], fmod_ref.at[req]
+    if not final:
+        x_ref = x_ref.at[req]
+    mine = refs[6:16]
+    theirs = refs[16:26]
+    stale = refs[26:29]
+    text_ref = refs[29]
     if final:
-        vel_ref, fresh_ref = refs[25:27]
-        scratch = refs[27:]
+        vel_ref, fresh_ref = refs[30:32]
+        scratch = refs[32:]
         (w_kv, w_q, w_o, kv, normed, qbuf, attn, ones, sems, x_out) = scratch
     else:
-        x_out, fresh_ref = refs[25:27]
-        scratch = refs[27:]
+        x_out, fresh_ref = refs[30:32]
+        scratch = refs[32:]
         (w_kv, w_q, w_o, kv, normed, qbuf, attn, ones, sems) = scratch
     row_of = lambda slot, j: pl.multiple_of(sc[1 + slot * 4 + j], 16)
 
+    def put(ref, at, cols, dst, slot, j, dst_cols, sem):
+        pltpu.make_async_copy(
+            ref.at[pl.ds(at, BLK), cols], dst.at[pl.ds(row_of(slot, j), BLK), dst_cols], sem
+        ).start()
+
     def spread_z(pieces, cols, dst, dst_cols, sem):
-        zs, zb, za, zl, zh = pieces[:5]
-        for j, ref in enumerate((zs, zb, za)):
+        block, opposite = pieces[:2]
+        put(block, 0, cols, dst, 0, 0, dst_cols, sem)
+        put(opposite, 0, cols, dst, 1, 0, dst_cols, sem)
+        for j, ref in enumerate(pieces[2:5]):
             for slot in range(2):
-                pltpu.make_async_copy(
-                    ref.at[pl.ds(slot * BLK, BLK), cols],
-                    dst.at[pl.ds(row_of(slot, j), BLK), dst_cols],
-                    sem,
-                ).start()
-        for slot, ref in enumerate((zl, zh)):
-            pltpu.make_async_copy(
-                ref.at[:, cols], dst.at[pl.ds(row_of(slot, 3), BLK), dst_cols], sem
-            ).start()
+                put(ref, slot * BLK, cols, dst, slot, j + 1, dst_cols, sem)
 
     def spread_x(pieces, dst, dst_cols, sem):
-        for slot in range(2):
-            for j in range(4):
-                pltpu.make_async_copy(
-                    pieces[5 + slot].at[pl.ds(j * BLK, BLK), :],
-                    dst.at[pl.ds(row_of(slot, j), BLK), dst_cols],
-                    sem,
-                ).start()
+        cols = pl.ds(0, XC)
+        put(pieces[0], 0, pl.ds(ZC, XC), dst, 0, 0, dst_cols, sem)
+        for j, ref in enumerate(pieces[5:8]):
+            put(ref, 0, cols, dst, 0, j + 1, dst_cols, sem)
+        for j in range(3):
+            put(pieces[8], j * BLK, cols, dst, 1, j, dst_cols, sem)
+        put(pieces[9], 0, cols, dst, 1, 3, dst_cols, sem)
 
     def fetch(kv_pieces, oq_pieces):
         spread_z(kv_pieces, pl.ds(0, ZC), w_kv, pl.ds(0, ZC), sems.at[0])
@@ -152,10 +169,11 @@
     def _():
         fetch(theirs, mine)
 
-    row = ROWS
-    for ref, count in ((st_b, ROWS), (st_a, ROWS), (st_l, ROWS // 2), (st_h, ROWS // 2), (text_ref, TXT_PAD)):
-        pltpu.make_async_copy(ref, kv.at[pl.ds(row, count), :], sems.at[3]).start()
-        row += count
+    for j, ref in enumerate((*stale, text_ref)):
+        count = ROWS if j < 3 else TXT_PAD
+        pltpu.make_async_copy(
+            ref.at[req], kv.at[pl.ds((j + 1) * ROWS, count), :], sems.at[3]
+        ).start()
 
     @pl.when(sc[0] == 0)
     def _():
@@ -270,7 +288,7 @@
         vel_ref[...] = jnp.dot(normed[...], fw_ref[...], preferred_element_type=jnp.float32)
 
 
-def run_layer(scalars, x, mod, fmod, gain, fw, mine, theirs, stale, text, final):
+def run_layer(scalars, x, mod, fmod, gain, fw, mine, theirs, stale, text, req, final):
     vmem = pl.BlockSpec(memory_space=pltpu.VMEM)
     hbm = pl.BlockSpec(memory_space=pl.ANY)
     first = (
@@ -292,10 +310,10 @@
     if final:
         scratch.append(pltpu.VMEM((ROWS, D), jnp.bfloat16))
     return pl.pallas_call(
-        lambda *refs: layer_kernel(final, *refs),
+        lambda *refs: layer_kernel(final, req, *refs),
         name="last_layer" if final else "first_layer",
         out_shape=(first, jax.ShapeDtypeStruct((ROWS, D), jnp.bfloat16)),
-        in_specs=[pl.BlockSpec(memory_space=pltpu.SMEM)] + [vmem] * 5 + [hbm] * 19,
+        in_specs=[pl.BlockSpec(memory_space=pltpu.SMEM)] + [vmem] * 5 + [hbm] * 24,
         out_specs=(vmem, vmem),
         scratch_shapes=scratch,
         compiler_params=pltpu.CompilerParams(vmem_limit_bytes=56 << 20),
@@ -320,21 +338,39 @@
     z_hi, x_at, core = shard // 8, (shard // 2) % 4, shard % 2
 
     qkv = qkv_weight[0]
-    half_kv = qkv[:, HW:]
     half_oq = jnp.concatenate([out_weight[0].T, qkv[:, :HW]], 1)
-    keep = jnp.where(core == 0, half_kv, half_oq)
-    give = jnp.where(core == 0, half_oq, half_kv)
-    got = core_flip(give)
-    block = jnp.concatenate(
-        [jnp.where(core == 0, keep, got), jnp.where(core == 0, got, keep)], 0
-    )
-    block_z, block_x = block[:, :ZC], block[:, ZC:]
-    pair_z = jnp.concatenate([block_z, z_flip(block_z)], 0)
-    four_x = jnp.concatenate([block_x, *ring_gather(block_x, x_shift)], 0)
-    mine = (pair_z, *ring_gather(pair_z, x_shift), four_x, z_flip(four_x))
-    theirs = tuple(core_flip(piece) for piece in mine)
-
-    stale = [ring_gather(stale_kv[0, r], y_shift) for r in range(2)]
+    both = jnp.stack([qkv[:, HW:], half_oq])
+    got = core_flip(both)
+    rows_of = jnp.where(core == 0, jnp.stack([both, got], 1), jnp.stack([got, both], 1))
+    rows_of = rows_of.reshape(2, BLK, D)
+    mine_block = jnp.where(core == 0, rows_of[0], rows_of[1])
+    their_block = jnp.where(core == 0, rows_of[1], rows_of[0])
+    near_z, near_x = mine_block[:, :ZC], mine_block[:, ZC:]
+
+    opposite_z = z_flip(near_z)
+    before_x, after_x = x_shift(near_x, 1), x_shift(near_x, -1)
+    before_y, after_y = y_shift(stale_kv[0], 1), y_shift(stale_kv[0], -1)
+    far_x = x_relay(jnp.where(core == 0, before_x, after_x))
+    opposite_x3 = z_flip(jnp.concatenate([after(near_x, opposite_z), before_x, after_x], 0))
+    pair_z = after(jnp.concatenate([near_z, opposite_z], 0), far_x)
+    before_z, after_z = x_shift(pair_z, 1), x_shift(pair_z, -1)
+    far_y = y_relay(jnp.where(core == 0, before_y, after_y))
+    their_far_x = core_flip(after(far_x, before_y))
+    their_before_x = core_flip(after(before_x, before_y))
+    their_after_x = core_flip(after(after_x, before_y))
+    far_z = x_relay(jnp.where(core == 0, before_z, after_z))
+    opposite_far = z_flip(after(far_x, opposite_x3))
+    their_opposite_z = core_flip(after(opposite_z, before_z))
+    their_before_z = core_flip(before_z)
+    their_after_z = core_flip(after_z)
+    their_opposite_x3 = core_flip(opposite_x3)
+    their_far_z = core_flip(far_z)
+    their_opposite_far = core_flip(opposite_far)
+    mine = (mine_block, opposite_z, before_z, after_z, far_z,
+            before_x, after_x, far_x, opposite_x3, opposite_far)
+    theirs = (their_block, their_opposite_z, their_before_z, their_after_z, their_far_z,
+              their_before_x, their_after_x, their_far_x, their_opposite_x3, their_opposite_far)
+    stale = (before_y, after_y, far_y)
     text = jnp.pad(text_kv[0], ((0, 0), (0, TXT_PAD - TXT), (0, 0)))
     gain = jnp.tile(score_gain[0] * (1.0 / math.sqrt(HEAD)), ZC // HEAD)[None, :]
     rows = [
@@ -344,13 +380,13 @@
 
     def layer(x, r, final):
         return run_layer(
-            scalars, x, modulation[0, r], final_mod[r], gain, final_weight,
-            mine, theirs, stale[r], text[r], final,
+            scalars, x, modulation[0], final_mod, gain, final_weight,
+            mine, theirs, stale, text, r, final,
         )
 
     fresh_first, arrived = [], []
     for r in range(2):
-        x_next, fresh = layer(hidden[r], r, False)
+        x_next, fresh = layer(hidden, r, False)
         fresh_first.append(fresh)
         arrived.append(lax.ppermute(x_next, "section", [(0, 1)]))
     fresh_out, velocity = [], []

time: 307 us -> 271 us (0.88)
  waiting for transfers between devices: 107 us -> 80.4 us
  starting transfers between devices: 43.8 us -> 32 us
  other arithmetic: 5.8 us -> 13.2 us
  local copies, waits for them, and re-layouts: 21.5 us -> 15.6 us
    ppermute x8 -> x2, waiting for transfers between devices: 55.4 us -> 10.9 us  [y_shift(): return lax.ppermute(value, 'patch', ring_pairs(dy))]
    ppermute x2 -> x3, waiting for transfers between devices: 0.36 us -> 28.3 us  [z_flip(): return lax.ppermute(value, 'shard', shard_pairs(flip_z=1))]
    ppermute x8 -> x4, waiting for transfers between devices: 46.1 us -> 26.8 us  [x_shift(): return lax.ppermute(value, 'shard', shard_pairs(dx=dx))]
    ppermute x8 -> x2, starting transfers between devices: 16.8 us -> 3.25 us  [y_shift(): return lax.ppermute(value, 'patch', ring_pairs(dy))]
    ppermute x0 -> x3, waiting for transfers between devices: none -> 10.4 us  [the longest x2 10.4 us: x_relay(): return lax.ppermute(value, 'shard', pairs)]
    ppermute x8 -> x4, starting transfers between devices: 11.7 us -> 6.54 us  [x_shift(): return lax.ppermute(value, 'shard', shard_pairs(dx=dx))]
    select_n x2 -> x5, other arithmetic: 2.61 us -> 6.54 us  [the longest x1 3.22 us: on_device(): jnp.where(core == 0, jnp.stack([both, got], 1), jnp.stack([got, both], 1))]
    squeeze x4 -> x0, local copies, waits for them, and re-layouts: 3.7 us -> none  [the longest x1 1.6 us: on_device(): x_next, fresh = layer(hidden[r], r, False)]
  transfers between devices with their start and end apart: 29 -> 25, of which waited for: 11 -> 13; matrix products, arithmetic and copies ran while one was open for 4% -> 6% of each run, Pallas kernels for 31% -> 24%
where the time goes in v2:
time: 271 us; the launch traced here: 270 us
  Pallas kernels  128 us (47%)
  waiting for transfers between devices  80.4 us (30%)
  starting transfers between devices  32 us (12%)
  local copies, waits for them, and re-layouts  15.6 us (6%)
  other arithmetic  13.2 us (5%)
    pallas_call x4, Pallas kernels, run_layer(): pl.pallas_call(lambda *refs: layer_kernel(final, req, *refs), name='last_...  128 us
    ppermute x3, waiting for transfers between devices, z_flip(): return lax.ppermute(value, 'shard', shard_pairs(flip_z=1))  28.3 us
    ppermute x4, waiting for transfers between devices, x_shift(): return lax.ppermute(value, 'shard', shard_pairs(dx=dx))  26.8 us
    unnamed x52, local copies, waits for them, and re-layouts  11.9 us
    ppermute x3, starting transfers between devices, z_flip(): return lax.ppermute(value, 'shard', shard_pairs(flip_z=1))  11.3 us
    ppermute x2, waiting for transfers between devices, y_shift(): return lax.ppermute(value, 'patch', ring_pairs(dy))  10.9 us
    ppermute x2, waiting for transfers between devices, x_relay(): return lax.ppermute(value, 'shard', pairs)  10.4 us
    ppermute x4, starting transfers between devices, x_shift(): return lax.ppermute(value, 'shard', shard_pairs(dx=dx))  6.54 us
  transfers between devices with their start and end apart: 25, of which 13 were waited for; matrix products, arithmetic and copies ran while one was open for 6% of the time, Pallas kernels for 24%

profile of v2, /device:TPU:0, one launch (start us, length us, event | category | flops | bytes accessed | tf_op | source)
XLA Modules:
  0.0 269.9 jit_solution(5049810832714745495)
XLA Ops:
  0.6 1.0 slice.38
  1.7 1.7 slice_bitcast_fusion
  3.4 1.8 fusion.3
  5.2 1.7 collective-permute-start.14
  6.8 1.6 collective-permute-start.20
  8.4 0.4 collective-permute-done
  8.8 3.2 %maximum_select_fusion = bf16[2,2,152,2432]{3,2,0,1:T(8,128)(2,1)S(1)} fusion(bf16[2,1,152,2432]{3,2,0,1:T(8,128)(2,1)} %bitcast.17, bf16[2,1,152,2432]{3,2,0,1:T(8,128)(2,1)} %get-tuple-element.40, pred[]{:T(512)S(6)} %eq.25), kind=kLoop, calls=%fused_computation | loop fusion | flops 4435968 | bytes 5914625 | tf_op jit(solution)/shard_map/jit(_where)/select_n | solution.py:344
  12.0 1.4 broadcast_select_fusion.2
  13.5 1.6 collective-permute-start.2
  15.1 1.7 collective-permute-start.3
  16.8 4.0 %collective-permute-start.1 = (bf16[304,1280]{1,0:T(8,128)(2,1)S(1)}, bf16[304,1280]{1,0:T(8,128)(2,1)S(1)}, u32[]{:S(2)}, u32[]{:S(2)}) collective-permute-start(bf16[304,1280]{1,0:T(8,128)(2,1)S(1)} %slice.41), channel_id=1, source_target_pairs={{0,8},{1,9},{2,10},{3,11},{4,12},{5,13},{6,14},{7,15},{8,0},{9,1},... | collective-permute-start | bytes 2334728 | tf_op jit(solution)/shard_map/ppermute | solution.py:53
  20.9 11.6 %collective-permute-done.2.refs_11_ = bf16[304,1152]{1,0:T(8,128)(2,1)S(1)} collective-permute-done((bf16[304,1152]{1,0:T(8,128)(2,1)S(1)}, bf16[304,1152]{1,0:T(8,128)(2,1)S(1)}, u32[]{:S(2)}, u32[]{:S(2)}) %collective-permute-start.2) | collective-permute-done | bytes 700448 | tf_op jit(solution)/shard_map/ppermute | solution.py:49
  32.7 1.6 collective-permute-start.4
  34.2 3.7 %collective-permute-done.1.refs_7_ = bf16[304,1280]{1,0:T(8,128)(2,1)S(1)} collective-permute-done((bf16[304,1280]{1,0:T(8,128)(2,1)S(1)}, bf16[304,1280]{1,0:T(8,128)(2,1)S(1)}, u32[]{:S(2)}, u32[]{:S(2)}) %collective-permute-start.1) | collective-permute-done | bytes 778272 | tf_op jit(solution)/shard_map/ppermute | solution.py:53
  38.0 0.1 pad_maximum_fusion.1
  38.1 6.9 %collective-permute-done.4.refs_13_ = bf16[304,1152]{1,0:T(8,128)(2,1)S(1)} collective-permute-done((bf16[304,1152]{1,0:T(8,128)(2,1)S(1)}, bf16[304,1152]{1,0:T(8,128)(2,1)S(1)}, u32[]{:S(2)}, u32[]{:S(2)}) %collective-permute-start.4) | collective-permute-done | bytes 700448 | tf_op jit(solution)/shard_map/ppermute | solution.py:71
  45.0 0.3 collective-permute-start.5
  45.3 3.0 %collective-permute-start.6 = (bf16[608,1280]{1,0:T(8,128)(2,1)S(1)}, bf16[608,1280]{1,0:T(8,128)(2,1)}, u32[]{:S(2)}, u32[]{:S(2)}) collective-permute-start(bf16[608,1280]{1,0:T(8,128)(2,1)S(1)} %pad_maximum_fusion.1), channel_id=1, source_target_pairs={{0,6},{1,7},{2,0},{3,1},{4,2},{5,3},{6,4},{7,5},{8,14},{9,15},{10,... | collective-permute-start | bytes 4669448 | tf_op jit(solution)/shard_map/ppermute | solution.py:49
  48.3 0.2 pad_maximum_fusion
  48.4 4.0 %collective-permute-start.8 = (bf16[912,1152]{1,0:T(8,128)(2,1)S(1)}, bf16[912,1152]{1,0:T(8,128)(2,1)}, u32[]{:S(2)}, u32[]{:S(2)}) collective-permute-start(bf16[912,1152]{1,0:T(8,128)(2,1)S(1)} %pad_maximum_fusion), channel_id=1, source_target_pairs={{0,8},{1,9},{2,10},{3,11},{4,12},{5,13},{6,14},{7,15},{8,0},{9,1},... | collective-permute-start | bytes 6303752 | tf_op jit(solution)/shard_map/ppermute | solution.py:53
  52.4 10.8 %collective-permute-done.14.refs_26_ = bf16[2,256,2432]{2,1,0:T(8,128)(2,1)S(1)} collective-permute-done((bf16[2,256,2432]{2,1,0:T(8,128)(2,1)}, bf16[2,256,2432]{2,1,0:T(8,128)(2,1)S(1)}, u32[]{:S(2)}, u32[]{:S(2)}) %collective-permute-start.14) | collective-permute-done | bytes 2490400 | tf_op jit(solution)/shard_map/ppermute | solution.py:61
  63.2 0.1 collective-permute-done.20.refs_27_
  63.3 0.3 broadcast_select_fusion
  63.6 1.1 copy-done
  64.7 0.6 collective-permute-start.21
  65.3 15.1 %collective-permute-done.5.refs_8_ = bf16[608,1280]{1,0:T(8,128)(2,1)} collective-permute-done((bf16[608,1280]{1,0:T(8,128)(2,1)S(1)}, bf16[608,1280]{1,0:T(8,128)(2,1)}, u32[]{:S(2)}, u32[]{:S(2)}) %collective-permute-start.5) | collective-permute-done | bytes 1556512 | tf_op jit(solution)/shard_map/ppermute | solution.py:49
  80.4 1.6 broadcast_select_fusion.1
  81.9 1.2 collective-permute-start.7
  83.1 0.5 collective-permute-start.16
  83.6 12.3 %collective-permute-done.8.refs_14_ = bf16[912,1152]{1,0:T(8,128)(2,1)} collective-permute-done((bf16[912,1152]{1,0:T(8,128)(2,1)S(1)}, bf16[912,1152]{1,0:T(8,128)(2,1)}, u32[]{:S(2)}, u32[]{:S(2)}) %collective-permute-start.8) | collective-permute-done | bytes 2101280 | tf_op jit(solution)/shard_map/ppermute | solution.py:53
  96.0 3.3 %collective-permute-start.9 = (bf16[304,1152]{1,0:T(8,128)(2,1)S(1)}, bf16[304,1152]{1,0:T(8,128)(2,1)}, u32[]{:S(2)}, u32[]{:S(2)}) collective-permute-start(bf16[304,1152]{1,0:T(8,128)(2,1)S(1)} %collective-permute-done.4.refs_13_), channel_id=1, source_target_pairs={{0,8},{1,9},{2,10},{3,11},{4,12},{5,13},{6,14},{7,15},{8,0},{9,1},... | collective-permute-start | bytes 2101256 | tf_op jit(solution)/shard_map/ppermute | solution.py:53
  99.3 0.2 collective-permute-start.18
  99.5 0.3 collective-permute-start.11
  99.8 0.2 collective-permute-start.12
  100.0 3.5 %collective-permute-done.7.refs_10_ = bf16[608,1280]{1,0:T(8,128)(2,1)} collective-permute-done((bf16[608,1280]{1,0:T(8,128)(2,1)S(1)}, bf16[608,1280]{1,0:T(8,128)(2,1)}, u32[]{:S(2)}, u32[]{:S(2)}) %collective-permute-start.7) | collective-permute-done | bytes 1556512 | tf_op jit(solution)/shard_map/ppermute | solution.py:71
  103.6 12.2 %collective-permute-done.9.refs_15_ = bf16[304,1152]{1,0:T(8,128)(2,1)} collective-permute-done((bf16[304,1152]{1,0:T(8,128)(2,1)S(1)}, bf16[304,1152]{1,0:T(8,128)(2,1)}, u32[]{:S(2)}, u32[]{:S(2)}) %collective-permute-start.9) | collective-permute-done | bytes 700448 | tf_op jit(solution)/shard_map/ppermute | solution.py:53
  115.8 2.3 collective-permute-done.10.refs_17_
  118.1 0.2 collective-permute-start.19
  118.3 1.5 copy.27
  119.8 0.7 broadcast_in_dim_tile.3.refs_4_
  120.5 1.1 copy.16.refs_5_
  121.6 1.5 copy.26
  123.1 1.3 pad.4.refs_29_
  124.4 0.6 stack.80.refs_0_
  125.1 1.4 copy-done.2
  126.4 30.9 %first_layer.3 = (bf16[256,2432]{1,0:T(8,128)(2,1)}, bf16[256,2432]{1,0:T(8,128)(2,1)}) custom-call(s32[9]{0:T(128)} %stack.80.refs_0_, bf16[2,256,2432]{2,1,0:T(8,128)(2,1)} %refs_1_.3, f32[2,3,2432]{2,1,0:T(4,128)} %bitcast.50, f32[2,2,2432]{2,1,0:T(2,128)} %refs_3_.7, f32[1,1280]{1,0:T(1,128)} %broadcast_in_dim_tile.3.refs_4_, ...), custom_call_target="tpu_custom_call" | custom-call | tf_op jit(solution)/shard_map/first_layer/pallas_call | solution.py:312
  157.4 3.4 %collective-permute-start.23 = (bf16[256,2432]{1,0:T(8,128)(2,1)}, bf16[256,2432]{1,0:T(8,128)(2,1)S(1)}, u32[]{:S(2)}, u32[]{:S(2)}) collective-permute-start(bf16[256,2432]{1,0:T(8,128)(2,1)} %get-tuple-element.29), channel_id=1, source_target_pairs={{0,64},{1,65},{2,66},{3,67},{4,68},{5,69},{6,70},{7,71},{8,72},{9,... | collective-permute-start | bytes 3735560 | tf_op jit(solution)/shard_map/ppermute | solution.py:391
  160.8 30.9 %first_layer.2 = (bf16[256,2432]{1,0:T(8,128)(2,1)}, bf16[256,2432]{1,0:T(8,128)(2,1)}) custom-call(s32[9]{0:T(128)} %stack.80.refs_0_, bf16[2,256,2432]{2,1,0:T(8,128)(2,1)} %refs_1_.3, f32[2,3,2432]{2,1,0:T(4,128)} %bitcast.51, f32[2,2,2432]{2,1,0:T(2,128)} %refs_3_.7, f32[1,1280]{1,0:T(1,128)} %broadcast_in_dim_tile.3.refs_4_, ...), custom_call_target="tpu_custom_call" | custom-call | tf_op jit(solution)/shard_map/first_layer/pallas_call | solution.py:312
  191.7 1.4 collective-permute-start.22
  193.1 0.1 copy.20
  193.3 1.1 copy-done.12
  194.4 32.9 %last_layer.3 = (f32[256,64]{1,0:T(8,128)}, bf16[256,2432]{1,0:T(8,128)(2,1)}) custom-call(s32[9]{0:T(128)} %stack.80.refs_0_, bf16[256,2432]{1,0:T(8,128)(2,1)} %copy-done.12, f32[2,3,2432]{2,1,0:T(4,128)} %bitcast.52, f32[2,2,2432]{2,1,0:T(2,128)} %refs_3_.7, f32[1,1280]{1,0:T(1,128)} %broadcast_in_dim_tile.3.refs_4_, bf16[2432,64]{1,0:T(8,128)(2,1)} %copy.16.refs_5_, ...), custom_call_target="tpu_custom_call" | custom-call | tf_op jit(solution)/shard_map/last_layer/pallas_call | solution.py:312
  227.3 1.1 copy-done.11
  228.4 33.0 %last_layer.2 = (f32[256,64]{1,0:T(8,128)}, bf16[256,2432]{1,0:T(8,128)(2,1)}) custom-call(s32[9]{0:T(128)} %stack.80.refs_0_, bf16[256,2432]{1,0:T(8,128)(2,1)} %copy-done.11, f32[2,3,2432]{2,1,0:T(4,128)} %bitcast.53, f32[2,2,2432]{2,1,0:T(2,128)} %refs_3_.7, f32[1,1280]{1,0:T(1,128)} %broadcast_in_dim_tile.3.refs_4_, bf16[2432,64]{1,0:T(8,128)(2,1)} %copy.16.refs_5_, ...), custom_call_target="tpu_custom_call" | custom-call | tf_op jit(solution)/shard_map/last_layer/pallas_call | solution.py:312
  261.4 0.9 fusion.1
  262.3 1.3 collective-permute-start.24
  263.6 0.1 select_bitcast_fusion
  263.7 1.1 copy-done.14
  264.9 0.4 copy-done.16
  265.2 0.1 select_bitcast_fusion.1
  265.4 1.7 maximum_bitcast_fusion
  267.1 1.3 collective-permute-done.24
  268.5 0.7 copy.22
  269.2 0.7 copy.23
  (65 shorter events, 0.5 us)
Async XLA Ops:
  5.2 3.6 %collective-permute-start = (bf16[2,152,2432]{2,1,0:T(8,128)(2,1)}, bf16[2,152,2432]{2,1,0:T(8,128)(2,1)}, u32[]{:S(2)}, u32[]{:S(2)}) collective-permute-start(bf16[2,152,2432]{2,1,0:T(8,128)(2,1)} %get-tuple-element.41), channel_id=1, source_target_pairs={{0,1},{1,0},{2,3},{3,2},{4,5},{5,4},{6,7},{7,6},{8,9},{9,8},{10,11... | collective-permute-start | bytes 4435976 | tf_op jit(solution)/shard_map/ppermute | solution.py:57
  5.2 58.0 %collective-permute-start.14 = (bf16[2,256,2432]{2,1,0:T(8,128)(2,1)}, bf16[2,256,2432]{2,1,0:T(8,128)(2,1)S(1)}, u32[]{:S(2)}, u32[]{:S(2)}) collective-permute-start(bf16[2,256,2432]{2,1,0:T(8,128)(2,1)} %bitcast.20), channel_id=1, source_target_pairs={{0,16},{16,32},{32,48},{48,0},{1,17},{17,33},{33,49},{49,1},{2,18}... | collective-permute-start | bytes 7471112 | tf_op jit(solution)/shard_map/ppermute | solution.py:61
  6.8 56.5 %collective-permute-start.20 = (bf16[2,256,2432]{2,1,0:T(8,128)(2,1)}, bf16[2,256,2432]{2,1,0:T(8,128)(2,1)}, u32[]{:S(2)}, u32[]{:S(2)}) collective-permute-start(bf16[2,256,2432]{2,1,0:T(8,128)(2,1)} %bitcast.20), channel_id=1, source_target_pairs={{0,48},{16,0},{32,16},{48,32},{1,49},{17,1},{33,17},{49,33},{2,50}... | collective-permute-start | bytes 7471112 | tf_op jit(solution)/shard_map/ppermute | solution.py:61
  13.4 19.3 %copy-start.1 = (bf16[1,2,152,2432]{3,2,0,1:T(8,128)(2,1)}, bf16[1,2,152,2432]{3,2,0,1:T(8,128)(2,1)S(1)}, u32[]{:S(2)}) copy-start(bf16[1,2,152,2432]{3,2,0,1:T(8,128)(2,1)S(1)} %get-tuple-element.39) | copy-start | bytes 4435972
  13.5 19.0 %collective-permute-start.2 = (bf16[304,1152]{1,0:T(8,128)(2,1)S(1)}, bf16[304,1152]{1,0:T(8,128)(2,1)S(1)}, u32[]{:S(2)}, u32[]{:S(2)}) collective-permute-start(bf16[304,1152]{1,0:T(8,128)(2,1)S(1)} %slice.42), channel_id=1, source_target_pairs={{0,2},{1,3},{2,4},{3,5},{4,6},{5,7},{6,0},{7,1},{8,10},{9,11},{10,... | collective-permute-start | bytes 2101256 | tf_op jit(solution)/shard_map/ppermute | solution.py:49
  15.1 17.5 %collective-permute-start.3 = (bf16[304,1152]{1,0:T(8,128)(2,1)S(1)}, bf16[304,1152]{1,0:T(8,128)(2,1)S(1)}, u32[]{:S(2)}, u32[]{:S(2)}) collective-permute-start(bf16[304,1152]{1,0:T(8,128)(2,1)S(1)} %slice.42), channel_id=1, source_target_pairs={{0,6},{1,7},{2,0},{3,1},{4,2},{5,3},{6,4},{7,5},{8,14},{9,15},{10,... | collective-permute-start | bytes 2101256 | tf_op jit(solution)/shard_map/ppermute | solution.py:49
  16.8 21.1 %collective-permute-start.1 = (bf16[304,1280]{1,0:T(8,128)(2,1)S(1)}, bf16[304,1280]{1,0:T(8,128)(2,1)S(1)}, u32[]{:S(2)}, u32[]{:S(2)}) collective-permute-start(bf16[304,1280]{1,0:T(8,128)(2,1)S(1)} %slice.41), channel_id=1, source_target_pairs={{0,8},{1,9},{2,10},{3,11},{4,12},{5,13},{6,14},{7,15},{8,0},{9,1},... | collective-permute-start | bytes 2334728 | tf_op jit(solution)/shard_map/ppermute | solution.py:53
  32.5 50.6 %copy-start.3 = (bf16[304,1152]{1,0:T(8,128)(2,1)}, bf16[304,1152]{1,0:T(8,128)(2,1)S(1)}, u32[]{:S(2)}) copy-start(bf16[304,1152]{1,0:T(8,128)(2,1)S(1)} %collective-permute-done.2.refs_11_) | copy-start | bytes 2101252
  32.6 50.6 %copy-start.4 = (bf16[304,1152]{1,0:T(8,128)(2,1)}, bf16[304,1152]{1,0:T(8,128)(2,1)S(1)}, u32[]{:S(2)}) copy-start(bf16[304,1152]{1,0:T(8,128)(2,1)S(1)} %collective-permute-done.3.refs_12_) | copy-start | bytes 2101252
  32.7 12.3 %collective-permute-start.4 = (bf16[304,1152]{1,0:T(8,128)(2,1)S(1)}, bf16[304,1152]{1,0:T(8,128)(2,1)S(1)}, u32[]{:S(2)}, u32[]{:S(2)}) collective-permute-start(bf16[304,1152]{1,0:T(8,128)(2,1)S(1)} %broadcast_select_fusion.4), channel_id=1, source_target_pairs={{0,2},{1,7},{2,4},{3,1},{4,6},{5,3},{6,0},{7,5},{8,10},{9,15},{10,... | collective-permute-start | bytes 2101256 | tf_op jit(solution)/shard_map/ppermute | solution.py:71
  38.0 77.8 %copy-start.5 = (bf16[304,1280]{1,0:T(8,128)(2,1)}, bf16[304,1280]{1,0:T(8,128)(2,1)S(1)}, u32[]{:S(2)}) copy-start(bf16[304,1280]{1,0:T(8,128)(2,1)S(1)} %collective-permute-done.1.refs_7_) | copy-start | bytes 2334724
  45.0 50.9 %copy-start.7 = (bf16[304,1152]{1,0:T(8,128)(2,1)}, bf16[304,1152]{1,0:T(8,128)(2,1)S(1)}, u32[]{:S(2)}) copy-start(bf16[304,1152]{1,0:T(8,128)(2,1)S(1)} %collective-permute-done.4.refs_13_) | copy-start | bytes 2101252
  45.0 35.3 %collective-permute-start.5 = (bf16[608,1280]{1,0:T(8,128)(2,1)S(1)}, bf16[608,1280]{1,0:T(8,128)(2,1)}, u32[]{:S(2)}, u32[]{:S(2)}) collective-permute-start(bf16[608,1280]{1,0:T(8,128)(2,1)S(1)} %pad_maximum_fusion.1), channel_id=1, source_target_pairs={{0,2},{1,3},{2,4},{3,5},{4,6},{5,7},{6,0},{7,1},{8,10},{9,11},{10,... | collective-permute-start | bytes 4669448 | tf_op jit(solution)/shard_map/ppermute | solution.py:49
  45.3 35.0 %collective-permute-start.6 = (bf16[608,1280]{1,0:T(8,128)(2,1)S(1)}, bf16[608,1280]{1,0:T(8,128)(2,1)}, u32[]{:S(2)}, u32[]{:S(2)}) collective-permute-start(bf16[608,1280]{1,0:T(8,128)(2,1)S(1)} %pad_maximum_fusion.1), channel_id=1, source_target_pairs={{0,6},{1,7},{2,0},{3,1},{4,2},{5,3},{6,4},{7,5},{8,14},{9,15},{10,... | collective-permute-start | bytes 4669448 | tf_op jit(solution)/shard_map/ppermute | solution.py:49
  48.4 47.5 %collective-permute-start.8 = (bf16[912,1152]{1,0:T(8,128)(2,1)S(1)}, bf16[912,1152]{1,0:T(8,128)(2,1)}, u32[]{:S(2)}, u32[]{:S(2)}) collective-permute-start(bf16[912,1152]{1,0:T(8,128)(2,1)S(1)} %pad_maximum_fusion), channel_id=1, source_target_pairs={{0,8},{1,9},{2,10},{3,11},{4,12},{5,13},{6,14},{7,15},{8,0},{9,1},... | collective-permute-start | bytes 6303752 | tf_op jit(solution)/shard_map/ppermute | solution.py:53
  63.2 1.4 copy-start
  64.7 55.2 %copy-start.21 = (f32[1,64]{1,0:T(1,128)S(1)}, f32[1,64]{1,0:T(1,128)}, u32[]{:S(2)}) copy-start(f32[1,64]{1,0:T(1,128)} %param.15) | copy-start | bytes 772
  64.7 55.8 %copy-start.19 = (bf16[2432,64]{0,1:T(8,128)(2,1)S(1)}, bf16[2432,64]{0,1:T(8,128)(2,1)}, u32[]{:S(2)}) copy-start(bf16[2432,64]{0,1:T(8,128)(2,1)} %param.19) | copy-start | bytes 933892
  64.7 35.2 %collective-permute-start.21 = (bf16[2,256,2432]{2,1,0:T(8,128)(2,1)S(1)}, bf16[2,256,2432]{2,1,0:T(8,128)(2,1)}, u32[]{:S(2)}, u32[]{:S(2)}) collective-permute-start(bf16[2,256,2432]{2,1,0:T(8,128)(2,1)S(1)} %broadcast_select_fusion), channel_id=1, source_target_pairs={{0,16},{1,49},{2,18},{3,51},{4,20},{5,53},{6,22},{7,55},{8,24},{9,... | collective-permute-start | bytes 7471112 | tf_op jit(solution)/shard_map/ppermute | solution.py:80
  81.9 21.6 %collective-permute-start.7 = (bf16[608,1280]{1,0:T(8,128)(2,1)S(1)}, bf16[608,1280]{1,0:T(8,128)(2,1)}, u32[]{:S(2)}, u32[]{:S(2)}) collective-permute-start(bf16[608,1280]{1,0:T(8,128)(2,1)S(1)} %broadcast_select_fusion.1), channel_id=1, source_target_pairs={{0,2},{1,7},{2,4},{3,1},{4,6},{5,3},{6,0},{7,5},{8,10},{9,15},{10,... | collective-permute-start | bytes 4669448 | tf_op jit(solution)/shard_map/ppermute | solution.py:71
  83.1 12.8 %collective-permute-start.15 = (bf16[304,1152]{1,0:T(8,128)(2,1)S(1)}, bf16[304,1152]{1,0:T(8,128)(2,1)S(1)}, u32[]{:S(2)}, u32[]{:S(2)}) collective-permute-start(bf16[304,1152]{1,0:T(8,128)(2,1)S(1)} %collective-permute-done.2.refs_11_), channel_id=1, source_target_pairs={{0,1},{1,0},{2,3},{3,2},{4,5},{5,4},{6,7},{7,6},{8,9},{9,8},{10,11... | collective-permute-start | bytes 2101256 | tf_op jit(solution)/shard_map/ppermute | solution.py:57
  83.1 16.2 %collective-permute-start.16 = (bf16[304,1152]{1,0:T(8,128)(2,1)S(1)}, bf16[304,1152]{1,0:T(8,128)(2,1)S(1)}, u32[]{:S(2)}, u32[]{:S(2)}) collective-permute-start(bf16[304,1152]{1,0:T(8,128)(2,1)S(1)} %collective-permute-done.3.refs_12_), channel_id=1, source_target_pairs={{0,1},{1,0},{2,3},{3,2},{4,5},{5,4},{6,7},{7,6},{8,9},{9,8},{10,11... | collective-permute-start | bytes 2101256 | tf_op jit(solution)/shard_map/ppermute | solution.py:57
  96.0 3.6 %collective-permute-start.17 = (bf16[304,1152]{1,0:T(8,128)(2,1)S(1)}, bf16[304,1152]{1,0:T(8,128)(2,1)S(1)}, u32[]{:S(2)}, u32[]{:S(2)}) collective-permute-start(bf16[304,1152]{1,0:T(8,128)(2,1)S(1)} %collective-permute-done.4.refs_13_), channel_id=1, source_target_pairs={{0,1},{1,0},{2,3},{3,2},{4,5},{5,4},{6,7},{7,6},{8,9},{9,8},{10,11... | collective-permute-start | bytes 2101256 | tf_op jit(solution)/shard_map/ppermute | solution.py:57
  96.0 22.1 %copy-start.8 = (bf16[304,1152]{1,0:T(8,128)(2,1)}, bf16[304,1152]{1,0:T(8,128)(2,1)S(1)}, u32[]{:S(2)}) copy-start(bf16[304,1152]{1,0:T(8,128)(2,1)S(1)} %collective-permute-done.15.refs_21_) | copy-start | bytes 2101252
  96.0 19.8 %collective-permute-start.9 = (bf16[304,1152]{1,0:T(8,128)(2,1)S(1)}, bf16[304,1152]{1,0:T(8,128)(2,1)}, u32[]{:S(2)}, u32[]{:S(2)}) collective-permute-start(bf16[304,1152]{1,0:T(8,128)(2,1)S(1)} %collective-permute-done.4.refs_13_), channel_id=1, source_target_pairs={{0,8},{1,9},{2,10},{3,11},{4,12},{5,13},{6,14},{7,15},{8,0},{9,1},... | collective-permute-start | bytes 2101256 | tf_op jit(solution)/shard_map/ppermute | solution.py:53
  99.3 18.7 %copy-start.9 = (bf16[304,1152]{1,0:T(8,128)(2,1)}, bf16[304,1152]{1,0:T(8,128)(2,1)S(1)}, u32[]{:S(2)}) copy-start(bf16[304,1152]{1,0:T(8,128)(2,1)S(1)} %collective-permute-done.16.refs_22_) | copy-start | bytes 2101252
  99.3 25.7 %collective-permute-start.18 = (bf16[912,1152]{1,0:T(8,128)(2,1)}, bf16[912,1152]{1,0:T(8,128)(2,1)S(1)}, u32[]{:S(2)}, u32[]{:S(2)}) collective-permute-start(bf16[912,1152]{1,0:T(8,128)(2,1)} %collective-permute-done.8.refs_14_), channel_id=1, source_target_pairs={{0,1},{1,0},{2,3},{3,2},{4,5},{5,4},{6,7},{7,6},{8,9},{9,8},{10,11... | collective-permute-start | bytes 6303752 | tf_op jit(solution)/shard_map/ppermute | solution.py:57
  99.5 18.5 %copy-start.10 = (bf16[304,1152]{1,0:T(8,128)(2,1)}, bf16[304,1152]{1,0:T(8,128)(2,1)S(1)}, u32[]{:S(2)}) copy-start(bf16[304,1152]{1,0:T(8,128)(2,1)S(1)} %collective-permute-done.17.refs_23_) | copy-start | bytes 2101252
  99.5 25.5 %collective-permute-start.11 = (bf16[608,1280]{1,0:T(8,128)(2,1)}, bf16[608,1280]{1,0:T(8,128)(2,1)}, u32[]{:S(2)}, u32[]{:S(2)}) collective-permute-start(bf16[608,1280]{1,0:T(8,128)(2,1)} %collective-permute-done.5.refs_8_), channel_id=1, source_target_pairs={{0,1},{1,0},{2,3},{3,2},{4,5},{5,4},{6,7},{7,6},{8,9},{9,8},{10,11... | collective-permute-start | bytes 4669448 | tf_op jit(solution)/shard_map/ppermute | solution.py:57
  99.8 25.2 %collective-permute-start.12 = (bf16[608,1280]{1,0:T(8,128)(2,1)}, bf16[608,1280]{1,0:T(8,128)(2,1)}, u32[]{:S(2)}, u32[]{:S(2)}) collective-permute-start(bf16[608,1280]{1,0:T(8,128)(2,1)} %collective-permute-done.6.refs_9_), channel_id=1, source_target_pairs={{0,1},{1,0},{2,3},{3,2},{4,5},{5,4},{6,7},{7,6},{8,9},{9,8},{10,11... | collective-permute-start | bytes 4669448 | tf_op jit(solution)/shard_map/ppermute | solution.py:57
  103.5 21.5 %collective-permute-start.13 = (bf16[608,1280]{1,0:T(8,128)(2,1)}, bf16[608,1280]{1,0:T(8,128)(2,1)}, u32[]{:S(2)}, u32[]{:S(2)}) collective-permute-start(bf16[608,1280]{1,0:T(8,128)(2,1)} %collective-permute-done.7.refs_10_), channel_id=1, source_target_pairs={{0,1},{1,0},{2,3},{3,2},{4,5},{5,4},{6,7},{7,6},{8,9},{9,8},{10,11... | collective-permute-start | bytes 4669448 | tf_op jit(solution)/shard_map/ppermute | solution.py:57
  115.8 2.3 collective-permute-start.10
  118.1 5.1 %copy-start.6 = (bf16[304,1280]{1,0:T(8,128)(2,1)}, bf16[304,1280]{1,0:T(8,128)(2,1)S(1)}, u32[]{:S(2)}) copy-start(bf16[304,1280]{1,0:T(8,128)(2,1)S(1)} %collective-permute-done.10.refs_17_) | copy-start | bytes 2334724
  118.1 7.0 %collective-permute-start.19 = (bf16[304,1152]{1,0:T(8,128)(2,1)}, bf16[304,1152]{1,0:T(8,128)(2,1)}, u32[]{:S(2)}, u32[]{:S(2)}) collective-permute-start(bf16[304,1152]{1,0:T(8,128)(2,1)} %collective-permute-done.9.refs_15_), channel_id=1, source_target_pairs={{0,1},{1,0},{2,3},{3,2},{4,5},{5,4},{6,7},{7,6},{8,9},{9,8},{10,11... | collective-permute-start | bytes 2101256 | tf_op jit(solution)/shard_map/ppermute | solution.py:57
  125.1 1.4 copy-start.2
  157.4 35.8 %copy-start.20 = (f32[2,128,64]{1,2,0:T(8,128)S(1)}, f32[2,128,64]{1,2,0:T(8,128)}, u32[]{:S(2)}) copy-start(f32[2,128,64]{1,2,0:T(8,128)} %param.20) | copy-start | bytes 196612
  157.4 35.9 %copy-start.22 = (s32[2]{0:T(128)S(1)}, s32[2]{0:T(128)}, u32[]{:S(2)}) copy-start(s32[2]{0:T(128)} %param.21) | copy-start | bytes 28
  157.4 35.9 %collective-permute-start.23 = (bf16[256,2432]{1,0:T(8,128)(2,1)}, bf16[256,2432]{1,0:T(8,128)(2,1)S(1)}, u32[]{:S(2)}, u32[]{:S(2)}) collective-permute-start(bf16[256,2432]{1,0:T(8,128)(2,1)} %get-tuple-element.29), channel_id=1, source_target_pairs={{0,64},{1,65},{2,66},{3,67},{4,68},{5,69},{6,70},{7,71},{8,72},{9,... | collective-permute-start | bytes 3735560 | tf_op jit(solution)/shard_map/ppermute | solution.py:391
  191.7 35.6 %collective-permute-start.22 = (bf16[256,2432]{1,0:T(8,128)(2,1)}, bf16[256,2432]{1,0:T(8,128)(2,1)S(1)}, u32[]{:S(2)}, u32[]{:S(2)}) collective-permute-start(bf16[256,2432]{1,0:T(8,128)(2,1)} %get-tuple-element.26), channel_id=1, source_target_pairs={{0,64},{1,65},{2,66},{3,67},{4,68},{5,69},{6,70},{7,71},{8,72},{9,... | collective-permute-start | bytes 3735560 | tf_op jit(solution)/shard_map/ppermute | solution.py:391
  193.3 1.1 copy-start.12
  227.3 34.1 %copy-start.17 = (f32[256,64]{1,0:T(8,128)S(1)}, f32[256,64]{1,0:T(8,128)}, u32[]{:S(2)}) copy-start(f32[256,64]{1,0:T(8,128)} %get-tuple-element.32) | copy-start | bytes 196612
  227.3 36.3 %copy-start.13 = (bf16[256,2432]{1,0:T(8,128)(2,1)S(1)}, bf16[256,2432]{1,0:T(8,128)(2,1)}, u32[]{:S(2)}) copy-start(bf16[256,2432]{1,0:T(8,128)(2,1)} %get-tuple-element.28) | copy-start | bytes 3735556
  227.3 36.3 %copy-start.15 = (bf16[256,2432]{1,0:T(8,128)(2,1)S(1)}, bf16[256,2432]{1,0:T(8,128)(2,1)}, u32[]{:S(2)}) copy-start(bf16[256,2432]{1,0:T(8,128)(2,1)} %get-tuple-element.30) | copy-start | bytes 3735556
  227.3 1.1 copy-start.11
  262.3 6.2 %collective-permute-start.24 = (bf16[2,128,64]{2,1,0:T(8,128)(2,1)S(1)}, bf16[2,128,64]{2,1,0:T(8,128)(2,1)S(1)}, u32[]{:S(2)}, u32[]{:S(2)}) collective-permute-start(bf16[2,128,64]{2,1,0:T(8,128)(2,1)S(1)} %fusion.1), channel_id=1, source_target_pairs={{64,0},{65,1},{66,2},{67,3},{68,4},{69,5},{70,6},{71,7},{72,8},{73... | collective-permute-start | bytes 98312 | tf_op jit(solution)/shard_map/ppermute | solution.py:399
  263.6 1.3 copy-start.14
  263.6 1.7 copy-start.16
  265.4 3.0 %copy-start.18 = (f32[256,64]{1,0:T(8,128)S(1)}, f32[256,64]{1,0:T(8,128)}, u32[]{:S(2)}) copy-start(f32[256,64]{1,0:T(8,128)} %get-tuple-element.31) | copy-start | bytes 196612
